TPU v7x, 32 devices: a whole 2x2x4 slice. The times are simulated.
32 devices in a mesh: ox: 4 (over y, core), oy: 8 (over z, x).
Axes of the slice: x: 2, y: 2, z: 4, core: 2. Of those that a mesh axis runs over, the one named last changes fastest.
Arguments:
- ocean_state: bfloat16 [512, 720, 256], P('oy', 'ox'), may hold values from -6 to 6
- diffusivity: float32 [512, 720], P('oy', 'ox'), may hold values from 0.04 to 0.24
- requests: int32 [32, 32, 2], P(('ox', 'oy')), may hold values from 0 to 89
- slot_ids: int32 [768, 16], P(('ox', 'oy')), may hold values from 0 to 63
- counts: int32 [768], P(('ox', 'oy')), may hold values from 1 to 16, as said below
- remap_weights: bfloat16 [768, 16, 128, 128], P(('ox', 'oy')), may hold values from -0.125 to 0.125
Outputs:
- atmosphere: bfloat16 [768, 128, 256], P(('ox', 'oy'))
Inputs may be any that keep to these rules, and one draw needn't show every extreme that they name: `counts`: at most 16; exactly 16 for some destination block in every draw.
All inputs are finite; a program needn't handle non-finite values.
Results may differ from a plain program's by a relative error of at most 0.0049.
Values may be sent and summed in bfloat16 or wider, within the bound.
No kernel may reach another device: no remote copies, remote signals or barrier semaphores. Data moves between devices by JAX's collectives and lax.ppermute only.
A program may use at most 128 MiB of HBM per device.

v0:
```python
import functools

import jax
import jax.numpy as jnp
from jax import lax
from jax.experimental import pallas as pl
from jax.experimental.pallas import tpu as pltpu
from jax.sharding import PartitionSpec as P

BLOCK = 128
LANES = 128
PACK = 16
AXES = ("ox", "oy")


def flatten_kernel(field_ref, *rest):
    out_ref, slabs, wide, rows32, sem = rest[-5:]
    pieces, columns, _, channels = slabs.shape
    halves = channels // LANES
    pitch = wide.shape[1] // columns
    margin = (out_ref.shape[0] - pieces * columns) // 2

    def fetch(piece):
        source = field_ref.at[:, pl.ds(pl.multiple_of(piece * PACK, PACK), PACK), :]
        return pltpu.make_async_copy(source, slabs.at[piece], sem.at[piece])

    @pl.loop(0, pieces)
    def _(piece):
        fetch(piece).start()

    @pl.loop(0, pieces)
    def _(piece):
        fetch(piece).wait()

        @pl.loop(0, columns, unroll=4)
        def _(column):
            value = slabs[piece, column].astype(jnp.float32)
            for half in range(halves):
                part = value[:, half * LANES : (half + 1) * LANES]
                wide[half, pl.ds(column * pitch, PACK), :] = part

        for row in range(PACK):
            for half in range(halves):
                picked = wide[half, pl.ds(row, columns, stride=pitch), :]
                rows32[half, pl.ds(row * columns, columns), :] = picked

        @pl.loop(0, columns, unroll=4)
        def _(step):
            base = pl.multiple_of(step * PACK, PACK)
            parts = [rows32[half, pl.ds(base, PACK), :] for half in range(halves)]
            out_ref[margin + piece * columns + step] = jnp.concatenate(parts, 1).astype(out_ref.dtype)


def flatten_cells(field, before):
    columns, rows, channels = field.shape
    pieces, halves = rows // PACK, channels // LANES
    margin = columns // PACK + 1
    return pl.pallas_call(
        flatten_kernel,
        out_shape=jax.ShapeDtypeStruct((pieces * columns + 2 * margin, PACK, channels), field.dtype),
        in_specs=[pl.BlockSpec(memory_space=pltpu.HBM)] + [pl.BlockSpec(memory_space=pl.ANY)] * len(before),
        out_specs=pl.BlockSpec(memory_space=pltpu.VMEM),
        scratch_shapes=[
            pltpu.VMEM((pieces, columns, PACK, channels), field.dtype),
            pltpu.VMEM((halves, columns * (PACK + 1), LANES), jnp.float32),
            pltpu.VMEM((halves, columns * PACK, LANES), jnp.float32),
            pltpu.SemaphoreType.DMA((pieces,)),
        ],
        compiler_params=pltpu.CompilerParams(vmem_limit_bytes=24 << 20),
        cost_estimate=pl.CostEstimate(flops=0, bytes_accessed=24 << 20, transcendentals=0),
        name="flatten",
    )(field, *before)


def smooth_kernel(masks, columns, rows, cap, asked, place, cells, coeff_ref, east_ref, west_ref, inner_ref, outer_ref, *rest):
    rest = rest[len(rest) - len(masks) - 8 :]
    outs = rest[: len(masks)]
    mid32, top32, bot32, rim_e, rim_w, rim_s, rim_n, made = rest[len(masks) :]
    channels = east_ref.shape[1]
    halves = channels // LANES
    me = place[0]
    up, shift = columns // PACK, columns % PACK
    margin = up + 1
    parts = ((-1, mid32), (up, top32), (-up - 1, bot32))

    def request(i):
        mask = masks[0]
        for j in range(1, len(masks)):
            mask = jnp.where(i // cap == j, masks[j], mask)
        return asked[me ^ mask, i % cap]

    odd, at_top = place[1] == 1, place[2] == 1
    for half in range(halves):
        lanes = pl.ds(half * LANES, LANES)
        rim_e[half] = east_ref[:, lanes].astype(jnp.float32)
        rim_w[half] = west_ref[:, lanes].astype(jnp.float32)
        inner, outer = inner_ref[:, lanes], outer_ref[:, lanes]
        rim_s[half] = jnp.where(odd, inner.astype(jnp.float32), outer.astype(jnp.float32))
        rim_n[half] = jnp.where(odd, outer.astype(jnp.float32), inner.astype(jnp.float32))

    @pl.when(at_top)
    def _():
        for half in range(halves):

            @pl.loop(0, columns // 2)
            def _(i):
                left = rim_n[half, pl.ds(i, 1), :]
                right = rim_n[half, pl.ds(columns - 1 - i, 1), :]
                rim_n[half, pl.ds(i, 1), :] = right
                rim_n[half, pl.ds(columns - 1 - i, 1), :] = left

    cell = lax.broadcasted_iota(jnp.int32, (BLOCK, LANES), 0)

    @pl.loop(0, len(masks) * cap)
    def _(i):
        block = request(i)
        for offset, wide in parts:
            for step in range(wide.shape[1] // PACK):
                value = cells[margin + block * (BLOCK // PACK) + offset + step].astype(jnp.float32)
                for half in range(halves):
                    part = value[:, half * LANES : (half + 1) * LANES]
                    wide[half, step * PACK : (step + 1) * PACK, :] = part
        total = rows * columns // BLOCK
        for n in range(pl.cdiv(columns, BLOCK)):
            low = n * BLOCK
            size = min(BLOCK, columns - low)

            @pl.when(block == n)
            def _():
                for half in range(halves):
                    bot32[half, PACK - shift : PACK - shift + size, :] = rim_s[half, low : low + size, :]

            begin = (total - 1 - n) * BLOCK - (rows - 1) * columns
            skip = max(0, -begin)

            @pl.when(block == total - 1 - n)
            def _():
                for half in range(halves):
                    top32[half, shift + skip : shift + BLOCK, :] = rim_n[half, begin + skip : begin + BLOCK, :]

        row = (block * BLOCK + columns - 1) // columns
        edge = row * columns - block * BLOCK
        row_w = jnp.minimum(row, rows - 1)
        row_e = jnp.maximum(row - 1, 0)
        scale = jnp.broadcast_to(coeff_ref[pl.ds(block, 1), :], (BLOCK, LANES)).T
        for half in range(halves):
            centre = mid32[half, PACK : PACK + BLOCK, :]
            east = mid32[half, PACK + 1 : PACK + 1 + BLOCK, :]
            west = mid32[half, PACK - 1 : PACK - 1 + BLOCK, :]
            north = top32[half, shift : shift + BLOCK, :]
            south = bot32[half, PACK - shift : PACK - shift + BLOCK, :]
            west = jnp.where(cell == edge, rim_w[half, pl.ds(row_w, 1), :], west)
            east = jnp.where(cell == edge - 1, rim_e[half, pl.ds(row_e, 1), :], east)
            beside = north + south + east + west
            value = centre + scale * (beside - 4.0 * centre)
            made[i, :, half * LANES : (half + 1) * LANES] = value.astype(made.dtype)

    for j, out in enumerate(outs):
        out[...] = made[j * cap : (j + 1) * cap]


def smooth_blocks(masks, asked, place, cells, coeff, east, west, inner, outer, before):
    channels = cells.shape[2]
    cap = asked.shape[1]
    count = len(masks) * cap
    run = BLOCK // PACK
    rows, columns = east.shape[0], inner.shape[0]
    anywhere = pl.BlockSpec(memory_space=pl.ANY)
    inside = pl.BlockSpec(memory_space=pltpu.VMEM)
    steps = (run + 2, run + 1, run + 1)
    halves = channels // LANES
    return pl.pallas_call(
        functools.partial(smooth_kernel, masks, columns, rows, cap),
        out_shape=[jax.ShapeDtypeStruct((cap, BLOCK, channels), cells.dtype)] * len(masks),
        grid_spec=pltpu.PrefetchScalarGridSpec(
            num_scalar_prefetch=2,
            grid=(),
            in_specs=[inside] * 6 + [anywhere] * len(before),
            out_specs=[inside] * len(masks),
            scratch_shapes=[pltpu.VMEM((halves, n * PACK, LANES), jnp.float32) for n in steps]
            + [pltpu.VMEM((halves, n, LANES), jnp.float32) for n in (rows, rows, columns, columns)]
            + [
                pltpu.VMEM((count, BLOCK, channels), cells.dtype),
            ],
        ),
        cost_estimate=pl.CostEstimate(
            flops=count * BLOCK * channels * 8,
            bytes_accessed=count * BLOCK * channels * 10,
            transcendentals=0,
        ),
        compiler_params=pltpu.CompilerParams(vmem_limit_bytes=12 << 20),
        name="smooth",
    )(asked, place, cells, coeff, east, west, inner, outer, *before)


def remap_kernel(masks, cap, slots, last, column, table, weights, *rest):
    arrived = rest[: len(masks)]
    rest = rest[len(masks) :]
    start_ref, ready = rest[:2] if last else (None, None)
    out_ref, *rest = rest[2 if last else 0 :]
    later = None if last else rest.pop(0)
    blocks, held, weight_sem, *made = rest
    dests, terms = held.shape[:2]
    me = table[0, table.shape[1] - 1]
    first = min(4, terms)
    bounds = [n for n in (8,) if n < terms] + [terms]

    def number(dest):
        return table[dest, column + terms]

    def used(dest):
        size = jnp.int32(first)
        low = first
        for bound in bounds:
            size = jnp.where(number(dest) > low, bound, size)
            low = bound
        return size

    def weight_copy(dest, place):
        term = table[dest, column + place] >> 16
        return pltpu.make_async_copy(weights.at[dest, term], held.at[dest, place], weight_sem.at[dest])

    begin = first if last else 0

    @pl.loop(0, dests)
    def _(dest):
        @pl.loop(begin, used(dest))
        def _(place):
            weight_copy(dest, place).start()

    def later_copy(dest, place):
        term = table[dest, column + terms + 1 + place] >> 16
        return pltpu.make_async_copy(weights.at[dest, term], later.at[dest, place], made[0].at[0])

    if not last:

        @pl.loop(0, dests)
        def _(dest):
            for place in range(first):
                later_copy(dest, place).start()

    blocks[slots] = jnp.zeros(blocks.shape[1:], blocks.dtype)
    for mask, ref in zip(masks, arrived):
        for c in range(cap):
            blocks[(me ^ mask) * cap + c] = ref[c]

    def product(dest, low, high):
        left = [ready[dest, g] if last and g < first else held[dest, g] for g in range(low, high)]
        right = [blocks[table[dest, column + g] & 65535] for g in range(low, high)]
        return jnp.dot(
            jnp.concatenate(left, 1), jnp.concatenate(right, 0), preferred_element_type=jnp.float32
        )

    def store(dest, value):
        if last:
            made[0][dest] = value.astype(made[0].dtype)
        else:
            out_ref[dest] = value

    def send(dest):
        return pltpu.make_async_copy(made[0].at[dest], out_ref.at[dest], made[1].at[0])

    together = 4 if dests % 4 == 0 else 1

    @pl.loop(0, dests // together)
    def _(group):
        for u in range(together):

            @pl.loop(begin, used(group * together + u))
            def _(place):
                weight_copy(group * together + u, place).wait()

        for u in range(together):
            dest = group * together + u
            value = product(dest, 0, first)
            store(dest, start_ref[dest] + value if last else value)
        for u in range(together):
            dest = group * together + u
            low = first
            for bound in bounds:

                @pl.when((number(dest) > low) & (number(dest) <= bound) if last else number(dest) > low)
                def _():
                    if last:
                        store(dest, start_ref[dest] + product(dest, 0, bound))
                    else:
                        store(dest, out_ref[dest] + product(dest, low, bound))

                low = bound
        if last:
            for u in range(together):
                send(group * together + u).start()

    @pl.loop(0, dests)
    def _(dest):
        if last:
            send(dest).wait()
        else:
            for place in range(first):
                later_copy(dest, place).wait()


def remap(masks, cap, slots, column, table, weights, arrived, start, dtype):
    dests, terms = weights.shape[:2]
    channels = arrived[0].shape[2]
    last = start is not None
    anywhere = pl.BlockSpec(memory_space=pl.ANY)
    inside = pl.BlockSpec(memory_space=pltpu.VMEM)
    shape = (dests, BLOCK, channels)
    result = jax.ShapeDtypeStruct(shape, dtype)
    ready = (dests, min(4, terms), BLOCK, BLOCK)
    return pl.pallas_call(
        functools.partial(remap_kernel, masks, cap, slots, last, column),
        out_shape=result if last else (result, jax.ShapeDtypeStruct(ready, weights.dtype)),
        grid_spec=pltpu.PrefetchScalarGridSpec(
            num_scalar_prefetch=1,
            grid=(),
            in_specs=[anywhere] + [inside] * (len(masks) + 2 * last),
            out_specs=anywhere if last else (inside, inside),
            scratch_shapes=[
                pltpu.VMEM((slots + 1, BLOCK, channels), arrived[0].dtype),
                pltpu.VMEM((dests, terms, BLOCK, BLOCK), weights.dtype),
                pltpu.SemaphoreType.DMA((dests,)),
            ]
            + ([pltpu.VMEM(shape, dtype)] if last else [])
            + [pltpu.SemaphoreType.DMA((1,))],
        ),
        compiler_params=pltpu.CompilerParams(vmem_limit_bytes=40 << 20),
        cost_estimate=pl.CostEstimate(
            flops=dests * terms * BLOCK * BLOCK * channels,
            bytes_accessed=weights.size,
            transcendentals=0,
        ),
        name="remap_last" if last else "remap_early",
    )(table, weights, *arrived, *(start if last else []))


def term_table(slot_ids, chosen, slots):
    terms = slot_ids.shape[1]
    index = jnp.arange(terms, dtype=jnp.int32)
    key = jnp.where(chosen, index[None, :], index[None, :] + terms)
    rank = jnp.sum(key[:, None, :] < key[:, :, None], axis=2)
    entry = index[None, :] * 65536 + jnp.where(chosen, slot_ids, slots)
    hit = rank[:, :, None] == index[None, None, :]
    ordered = jnp.sum(jnp.where(hit, entry[:, :, None], 0), axis=1)
    number = jnp.sum(chosen, axis=1, dtype=jnp.int32)[:, None]
    return [ordered, number]


def body(ocean_state, diffusivity, requests, slot_ids, counts, remap_weights):
    n_ox, n_oy = lax.axis_size("ox"), lax.axis_size("oy")
    devices = n_ox * n_oy
    rows, _, _ = ocean_state.shape
    cap = requests.shape[2]
    slots = devices * cap
    ox, oy = lax.axis_index("ox"), lax.axis_index("oy")
    me = (ox * n_oy + oy).astype(jnp.int32)
    assert devices & (devices - 1) == 0 and n_oy % 2 == 0 and rows % PACK == 0

    asked = lax.all_to_all(requests[0], AXES, split_axis=0, concat_axis=0, tiled=True)
    field = jnp.transpose(ocean_state, (1, 0, 2))
    held_field = pltpu.with_memory_space_constraint(field, pltpu.HBM)
    ring = [(i, (i + 1) % n_ox) for i in range(n_ox)]
    west = lax.ppermute(field[-1], "ox", ring)
    east = lax.ppermute(field[0], "ox", [(j, i) for i, j in ring])
    first_row, last_row = ocean_state[0], ocean_state[-1]
    odd = oy % 2 == 1
    top = n_oy - 1
    pairs = [(ox_ * n_oy + i, ox_ * n_oy + (i ^ 1)) for ox_ in range(n_ox) for i in range(n_oy)]
    inner = lax.ppermute(jnp.where(odd, first_row, last_row), AXES, pairs)
    pairs = [(i * n_oy + top, (n_ox - 1 - i) * n_oy + top) for i in range(n_ox)]
    for i in range(1, top, 2):
        for ox_ in range(n_ox):
            base = ox_ * n_oy + i
            pairs += [(base, base + 1), (base + 1, base)]
    outer = lax.ppermute(jnp.where(odd, last_row, first_row), AXES, pairs)

    coeff = diffusivity.reshape(-1, BLOCK)
    cells = flatten_cells(held_field, (coeff, asked))
    place = jnp.stack([me, odd.astype(jnp.int32), (oy == top).astype(jnp.int32)])

    half = n_oy // 2
    across = [m for m in range(devices) if m & half]
    beside = [m for m in range(devices) if not m & half]
    lead = 4
    order = across[:lead]
    for i, m in enumerate(beside[1:] + [beside[0]]):
        order += [m] + across[lead + i : lead + i + 1]
    late = across[-max(1, min(7, len(across) * 7 // 16)) :]
    order = [m for m in order if m not in late] + late
    groups = [order[:lead]] + [order[i : i + 10] for i in range(lead, devices, 10)]
    arrived, before = {}, []
    for number, group in enumerate(groups):
        made = smooth_blocks(tuple(group), asked, place, cells, coeff, east, west, inner, outer, before)
        if number == len(groups) - 1:
            slot_ids, counts, made = lax.optimization_barrier((slot_ids, counts, made))
        before = made[:1]
        for m, blocks in zip(group, made):
            pairs = [(i, i ^ m) for i in range(devices)]
            arrived[m] = lax.ppermute(blocks, AXES, pairs) if m else blocks

    term_total = slot_ids.shape[1]
    live = jnp.arange(term_total, dtype=jnp.int32)[None, :] < counts[:, None]
    offset = me ^ (slot_ids // cap)
    is_late = functools.reduce(jnp.logical_or, [offset == m for m in late])
    early = [m for m in order if m not in late]
    parts = term_table(slot_ids, live & ~is_late, slots) + term_table(slot_ids, live & is_late, slots)
    table = jnp.concatenate(parts + [jnp.full_like(parts[1], me)], axis=1)
    partial = remap(tuple(early), cap, slots, 0, table, remap_weights, [arrived[m] for m in early], None, jnp.float32)
    return remap(
        tuple(late), cap, slots, term_total + 1, table, remap_weights, [arrived[m] for m in late], partial, jnp.bfloat16
    )


def solution(mesh):
    placed = (
        P("oy", "ox", None),
        P("oy", "ox"),
        P(("ox", "oy"), None, None),
        P(("ox", "oy"), None),
        P(("ox", "oy")),
        P(("ox", "oy"), None, None, None),
    )
    return jax.shard_map(body, mesh=mesh, in_specs=placed, out_specs=P(("ox", "oy"), None, None), check_vma=False)
```

profile of v0, /device:TPU:0, one launch (start us, length us, event | category | flops | bytes accessed | tf_op | source)
XLA Modules:
  0.0 162.9 jit_solution(14398420104435061792)
XLA Ops:
  0.0 1.6 %fusion.5 = (bf16[1,180,256]{2,0,1:T(2,128)(2,1)S(1)}, bf16[1,180,256]{2,0,1:T(2,128)(2,1)S(1)}) fusion(bf16[64,180,256]{2,0,1:T(8,128)(2,1)} %param.6), kind=kLoop, calls=%fused_computation.31 | loop fusion | bytes 368640 | tf_op jit(solution)/shard_map/slice | solution.py:366
  1.7 3.0 %collective-permute-start.2 = (bf16[180,256]{1,0:T(8,128)(2,1)S(1)}, bf16[180,256]{1,0:T(8,128)(2,1)S(1)}, u32[]{:S(2)}, u32[]{:S(2)}) collective-permute-start(bf16[180,256]{1,0:T(8,128)(2,1)S(1)} %get-tuple-element.102), channel_id=1, source_target_pairs={{0,1},{1,0},{2,3},{3,2},{4,5},{5,4},{6,7},{7,6},{8,9},{9,8},{10,11... | collective-permute-start | bytes 276488 | tf_op jit(solution)/shard_map/ppermute | solution.py:370
  5.4 1.4 copy.39
  6.7 7.6 %all-to-all-start = ((s32[32,1,2]{2,1,0:T(1,128)}), s32[32,1,2]{2,1,0:T(1,128)S(1)}, u32[]{:S(2)}, u32[]{:S(2)}) async-start(s32[32,1,2]{2,1,0:T(1,128)} %copy.39), calls=%async_computation | async-start | bytes 32768 | tf_op jit(solution)/shard_map/all_to_all | solution.py:360
  14.4 0.8 slice_bitcast_fusion
  15.2 1.5 collective-permute-start
  16.7 1.0 reshape.29.rest_0_.coeff_ref
  17.7 3.7 %all-to-all-done = s32[32,1,2]{2,1,0:T(1,128)S(1)} async-done(((s32[32,1,2]{2,1,0:T(1,128)}), s32[32,1,2]{2,1,0:T(1,128)S(1)}, u32[]{:S(2)}, u32[]{:S(2)}) %all-to-all-start) | async-done | bytes 288 | tf_op jit(solution)/shard_map/all_to_all | solution.py:360
  21.4 5.3 %flatten.1.cells = bf16[744,16,256]{2,1,0:T(8,128)(2,1)S(1)} custom-call(bf16[180,64,256]{2,1,0:T(8,128)(2,1)} %bitcast.22, f32[90,128]{1,0:T(8,128)S(1)} %reshape.29.rest_0_.coeff_ref, s32[32,2]{1,0:T(8,128)S(1)} %bitcast.16), custom_call_target="tpu_custom_call" | custom-call | bytes 25165824 | tf_op jit(solution)/shard_map/flatten/pallas_call | solution.py:58
  26.8 2.9 %smooth.4 = (bf16[2,128,256]{2,1,0:T(8,128)(2,1)S(1)}, bf16[2,128,256]{2,1,0:T(8,128)(2,1)}, bf16[2,128,256]{2,1,0:T(8,128)(2,1)}, bf16[2,128,256]{2,1,0:T(8,128)(2,1)}) custom-call(s32[32,2]{1,0:T(8,128)S(1)} %bitcast.17, s32[3]{0:T(128)S(1)} %pad_add_fusion.place, bf16[744,16,256]{2,1,0:T(8,128)(2,1)S(1)} %flatten.1.cells, ...), custom_call_target="tpu_custom_call" | custom-call | flops 2097152 | bytes 2621440 | tf_op jit(solution)/shard_map/smooth/pallas_call | solution.py:172
  29.6 4.2 %smooth.5 = (bf16[2,128,256]{2,1,0:T(8,128)(2,1)S(1)}, bf16[2,128,256]{2,1,0:T(8,128)(2,1)S(1)}, bf16[2,128,256]{2,1,0:T(8,128)(2,1)S(1)}, bf16[2,128,256]{2,1,0...) custom-call(s32[32,2]{1,0:T(8,128)S(1)} %bitcast.18, ...), custom_call_target="tpu_custom_call" | custom-call | flops 5242880 | bytes 6553600 | tf_op jit(solution)/shard_map/smooth/pallas_call | solution.py:172
  33.9 4.2 %smooth.6 = (bf16[2,128,256]{2,1,0:T(8,128)(2,1)S(1)}, bf16[2,128,256]{2,1,0:T(8,128)(2,1)S(1)}, bf16[2,128,256]{2,1,0:T(8,128)(2,1)S(1)}, bf16[2,128,256]{2,1,0...) custom-call(s32[32,2]{1,0:T(8,128)S(1)} %bitcast.19, ...), custom_call_target="tpu_custom_call" | custom-call | flops 5242880 | bytes 6553600 | tf_op jit(solution)/shard_map/smooth/pallas_call | solution.py:172
  38.2 1.8 %collective-permute-start.26 = (bf16[2,128,256]{2,1,0:T(8,128)(2,1)S(1)}, bf16[2,128,256]{2,1,0:T(8,128)(2,1)S(1)}, u32[]{:S(2)}, u32[]{:S(2)}) collective-permute-start(bf16[2,128,256]{2,1,0:T(8,128)(2,1)S(1)} %get-tuple-element.81), channel_id=1, source_target_pairs={{0,11},{1,10},{2,9},{3,8},{4,15},{5,14},{6,13},{7,12},{8,3},{9,2},... | collective-permute-start | bytes 393224 | tf_op jit(solution)/shard_map/ppermute | solution.py:400
  40.6 2.3 %collective-permute-start.28 = (bf16[2,128,256]{2,1,0:T(8,128)(2,1)S(1)}, bf16[2,128,256]{2,1,0:T(8,128)(2,1)S(1)}, u32[]{:S(2)}, u32[]{:S(2)}) collective-permute-start(bf16[2,128,256]{2,1,0:T(8,128)(2,1)S(1)} %get-tuple-element.83), channel_id=1, source_target_pairs={{0,17},{1,16},{2,19},{3,18},{4,21},{5,20},{6,23},{7,22},{8,25},{9,... | collective-permute-start | bytes 393224 | tf_op jit(solution)/shard_map/ppermute | solution.py:400
  44.0 1.9 %collective-permute-start.30 = (bf16[2,128,256]{2,1,0:T(8,128)(2,1)S(1)}, bf16[2,128,256]{2,1,0:T(8,128)(2,1)S(1)}, u32[]{:S(2)}, u32[]{:S(2)}) collective-permute-start(bf16[2,128,256]{2,1,0:T(8,128)(2,1)S(1)} %get-tuple-element.85), channel_id=1, source_target_pairs={{0,19},{1,18},{2,17},{3,16},{4,23},{5,22},{6,21},{7,20},{8,27},{9,... | collective-permute-start | bytes 393224 | tf_op jit(solution)/shard_map/ppermute | solution.py:400
  45.9 1.1 collective-permute-done.26.rest_15_
  46.9 1.4 collective-permute-start.15
  48.3 6.7 %collective-permute-done.28.rest_17_ = bf16[2,128,256]{2,1,0:T(8,128)(2,1)S(1)} collective-permute-done((bf16[2,128,256]{2,1,0:T(8,128)(2,1)S(1)}, bf16[2,128,256]{2,1,0:T(8,128)(2,1)S(1)}, u32[]{:S(2)}, u32[]{:S(2)}) %collective-permute-start.28) | collective-permute-done | bytes 131104 | tf_op jit(solution)/shard_map/ppermute | solution.py:400
  55.1 1.6 %collective-permute-start.33 = (bf16[2,128,256]{2,1,0:T(8,128)(2,1)S(1)}, bf16[2,128,256]{2,1,0:T(8,128)(2,1)S(1)}, u32[]{:S(2)}, u32[]{:S(2)}) collective-permute-start(bf16[2,128,256]{2,1,0:T(8,128)(2,1)S(1)} %get-tuple-element.88), channel_id=1, source_target_pairs={{0,26},{1,27},{2,24},{3,25},{4,30},{5,31},{6,28},{7,29},{8,18},{9,... | collective-permute-start | bytes 393224 | tf_op jit(solution)/shard_map/ppermute | solution.py:400
  56.7 1.3 collective-permute-start.34
  58.0 4.1 %smooth.7 = (bf16[2,128,256]{2,1,0:T(8,128)(2,1)S(1)}, bf16[2,128,256]{2,1,0:T(8,128)(2,1)}, bf16[2,128,256]{2,1,0:T(8,128)(2,1)S(1)}, bf16[2,128,256]{2,1,0:T(8...) custom-call(s32[32,2]{1,0:T(8,128)S(1)} %bitcast.20, ...), custom_call_target="tpu_custom_call" | custom-call | flops 4194304 | bytes 5242880 | tf_op jit(solution)/shard_map/smooth/pallas_call | solution.py:172
  64.9 3.6 %collective-permute-start.16 = (bf16[2,128,256]{2,1,0:T(8,128)(2,1)S(1)}, bf16[2,128,256]{2,1,0:T(8,128)(2,1)S(1)}, u32[]{:S(2)}, u32[]{:S(2)}) collective-permute-start(bf16[2,128,256]{2,1,0:T(8,128)(2,1)S(1)} %get-tuple-element.72), channel_id=1, source_target_pairs={{0,12},{1,13},{2,14},{3,15},{4,8},{5,9},{6,10},{7,11},{8,4},{9,5},... | collective-permute-start | bytes 393224 | tf_op jit(solution)/shard_map/ppermute | solution.py:400
  68.5 3.9 %collective-permute-start.17 = (bf16[2,128,256]{2,1,0:T(8,128)(2,1)S(1)}, bf16[2,128,256]{2,1,0:T(8,128)(2,1)S(1)}, u32[]{:S(2)}, u32[]{:S(2)}) collective-permute-start(bf16[2,128,256]{2,1,0:T(8,128)(2,1)S(1)} %get-tuple-element.73), channel_id=1, source_target_pairs={{0,2},{1,3},{2,0},{3,1},{4,6},{5,7},{6,4},{7,5},{8,10},{9,11},{10,... | collective-permute-start | bytes 393224 | tf_op jit(solution)/shard_map/ppermute | solution.py:400
  72.5 1.0 collective-permute-start.19
  73.4 3.7 %collective-permute-start.20 = (bf16[2,128,256]{2,1,0:T(8,128)(2,1)S(1)}, bf16[2,128,256]{2,1,0:T(8,128)(2,1)S(1)}, u32[]{:S(2)}, u32[]{:S(2)}) collective-permute-start(bf16[2,128,256]{2,1,0:T(8,128)(2,1)S(1)} %get-tuple-element.76), channel_id=1, source_target_pairs={{0,14},{1,15},{2,12},{3,13},{4,10},{5,11},{6,8},{7,9},{8,6},{9,7},... | collective-permute-start | bytes 393224 | tf_op jit(solution)/shard_map/ppermute | solution.py:400
  77.3 2.2 %collective-permute-done.17.rest_6_ = bf16[2,128,256]{2,1,0:T(8,128)(2,1)S(1)} collective-permute-done((bf16[2,128,256]{2,1,0:T(8,128)(2,1)S(1)}, bf16[2,128,256]{2,1,0:T(8,128)(2,1)S(1)}, u32[]{:S(2)}, u32[]{:S(2)}) %collective-permute-start.17) | collective-permute-done | bytes 131104 | tf_op jit(solution)/shard_map/ppermute | solution.py:400
  79.5 2.9 %collective-permute-done.18.rest_7_ = bf16[2,128,256]{2,1,0:T(8,128)(2,1)S(1)} collective-permute-done((bf16[2,128,256]{2,1,0:T(8,128)(2,1)S(1)}, bf16[2,128,256]{2,1,0:T(8,128)(2,1)S(1)}, u32[]{:S(2)}, u32[]{:S(2)}) %collective-permute-start.18) | collective-permute-done | bytes 131104 | tf_op jit(solution)/shard_map/ppermute | solution.py:400
  82.4 3.0 %collective-permute-start.22 = (bf16[2,128,256]{2,1,0:T(8,128)(2,1)S(1)}, bf16[2,128,256]{2,1,0:T(8,128)(2,1)S(1)}, u32[]{:S(2)}, u32[]{:S(2)}) collective-permute-start(bf16[2,128,256]{2,1,0:T(8,128)(2,1)S(1)} %get-tuple-element.78), channel_id=1, source_target_pairs={{0,15},{1,14},{2,13},{3,12},{4,11},{5,10},{6,9},{7,8},{8,7},{9,6},... | collective-permute-start | bytes 393224 | tf_op jit(solution)/shard_map/ppermute | solution.py:400
  85.5 1.7 %collective-permute-start.23 = (bf16[2,128,256]{2,1,0:T(8,128)(2,1)S(1)}, bf16[2,128,256]{2,1,0:T(8,128)(2,1)S(1)}, u32[]{:S(2)}, u32[]{:S(2)}) collective-permute-start(bf16[2,128,256]{2,1,0:T(8,128)(2,1)S(1)} %get-tuple-element.79), channel_id=1, source_target_pairs={{0,9},{1,8},{2,11},{3,10},{4,13},{5,12},{6,15},{7,14},{8,1},{9,0},... | collective-permute-start | bytes 393224 | tf_op jit(solution)/shard_map/ppermute | solution.py:400
  87.2 7.6 %collective-permute-start.24 = (bf16[2,128,256]{2,1,0:T(8,128)(2,1)S(1)}, bf16[2,128,256]{2,1,0:T(8,128)(2,1)S(1)}, u32[]{:S(2)}, u32[]{:S(2)}) collective-permute-start(bf16[2,128,256]{2,1,0:T(8,128)(2,1)S(1)} %get-tuple-element.80), channel_id=1, source_target_pairs={{0,20},{1,21},{2,22},{3,23},{4,16},{5,17},{6,18},{7,19},{8,28},{9,... | collective-permute-start | bytes 393224 | tf_op jit(solution)/shard_map/ppermute | solution.py:400
  95.5 0.7 collective-permute-start.12
  96.2 1.1 collective-permute-start.13
  97.3 3.1 %collective-permute-start.14 = (bf16[2,128,256]{2,1,0:T(8,128)(2,1)}, bf16[2,128,256]{2,1,0:T(8,128)(2,1)}, u32[]{:S(2)}, u32[]{:S(2)}) collective-permute-start(bf16[2,128,256]{2,1,0:T(8,128)(2,1)} %get-tuple-element.71), channel_id=1, source_target_pairs={{0,7},{1,6},{2,5},{3,4},{4,3},{5,2},{6,1},{7,0},{8,15},{9,14},{10,... | collective-permute-start | bytes 393224 | tf_op jit(solution)/shard_map/ppermute | solution.py:400
  100.3 12.9 %collective-permute-done.24.rest_13_ = bf16[2,128,256]{2,1,0:T(8,128)(2,1)S(1)} collective-permute-done((bf16[2,128,256]{2,1,0:T(8,128)(2,1)S(1)}, bf16[2,128,256]{2,1,0:T(8,128)(2,1)S(1)}, u32[]{:S(2)}, u32[]{:S(2)}) %collective-permute-start.24) | collective-permute-done | bytes 131104 | tf_op jit(solution)/shard_map/ppermute | solution.py:400
  113.2 3.5 %collective-permute-start.10 = (bf16[2,128,256]{2,1,0:T(8,128)(2,1)}, bf16[2,128,256]{2,1,0:T(8,128)(2,1)S(1)}, u32[]{:S(2)}, u32[]{:S(2)}) collective-permute-start(bf16[2,128,256]{2,1,0:T(8,128)(2,1)} %get-tuple-element.68), channel_id=1, source_target_pairs={{0,31},{1,30},{2,29},{3,28},{4,27},{5,26},{6,25},{7,24},{8,23},{9,... | collective-permute-start | bytes 393224 | tf_op jit(solution)/shard_map/ppermute | solution.py:400
  116.8 0.7 copy.48
  118.1 1.3 copy.49
  119.4 1.3 copy.51
  121.3 0.9 concatenate.3.table
  122.2 1.9 %collective-permute-start.5 = (bf16[2,128,256]{2,1,0:T(8,128)(2,1)}, bf16[2,128,256]{2,1,0:T(8,128)(2,1)S(1)}, u32[]{:S(2)}, u32[]{:S(2)}) collective-permute-start(bf16[2,128,256]{2,1,0:T(8,128)(2,1)} %copy-done.3), channel_id=1, source_target_pairs={{0,22},{1,23},{2,20},{3,21},{4,18},{5,19},{6,16},{7,17},{8,30},{9,... | collective-permute-start | bytes 393224 | tf_op jit(solution)/shard_map/ppermute | solution.py:400
  124.1 3.2 %collective-permute-start.6 = (bf16[2,128,256]{2,1,0:T(8,128)(2,1)}, bf16[2,128,256]{2,1,0:T(8,128)(2,1)S(1)}, u32[]{:S(2)}, u32[]{:S(2)}) collective-permute-start(bf16[2,128,256]{2,1,0:T(8,128)(2,1)} %copy-done.2), channel_id=1, source_target_pairs={{0,23},{1,22},{2,21},{3,20},{4,19},{5,18},{6,17},{7,16},{8,31},{9,... | collective-permute-start | bytes 393224 | tf_op jit(solution)/shard_map/ppermute | solution.py:400
  127.3 1.6 collective-permute-start.7
  128.9 12.5 %collective-permute-start.8 = (bf16[2,128,256]{2,1,0:T(8,128)(2,1)}, bf16[2,128,256]{2,1,0:T(8,128)(2,1)S(1)}, u32[]{:S(2)}, u32[]{:S(2)}) collective-permute-start(bf16[2,128,256]{2,1,0:T(8,128)(2,1)} %copy-done), channel_id=1, source_target_pairs={{0,29},{1,28},{2,31},{3,30},{4,25},{5,24},{6,27},{7,26},{8,21},{9,... | collective-permute-start | bytes 393224 | tf_op jit(solution)/shard_map/ppermute | solution.py:400
  141.4 3.1 %collective-permute-start.9 = (bf16[2,128,256]{2,1,0:T(8,128)(2,1)S(1)}, bf16[2,128,256]{2,1,0:T(8,128)(2,1)S(1)}, u32[]{:S(2)}, u32[]{:S(2)}) collective-permute-start(bf16[2,128,256]{2,1,0:T(8,128)(2,1)S(1)} %get-tuple-element.67), channel_id=1, source_target_pairs={{0,30},{1,31},{2,28},{3,29},{4,26},{5,27},{6,24},{7,25},{8,22},{9,... | collective-permute-start | bytes 393224 | tf_op jit(solution)/shard_map/ppermute | solution.py:400
  144.4 6.5 %remap_early.1 = (f32[24,128,256]{2,1,0:T(8,128)S(1)}, bf16[24,4,128,128]{3,2,1,0:T(8,128)(2,1)S(1)}) custom-call(s32[24,35]{1,0:T(8,128)S(1)} %concatenate.3.table, bf16[24,16,128,128]{3,2,1,0:T(8,128)(2,1)} %weights.3, bf16[2,128,256]{2,1,0:T(8,128)(2,1)S(1)} %collective-permute-done.11.rest_0_, bf16[2,128,256]{2,1,0:T(8,128)(2,1)S(1)} %collective-permute-done.12.rest_1_, ...), custom_call_target="tpu_custom_call" | custom-call | flops 1610612736 | bytes 6291456 | tf_op jit(solution)/shard_map/remap_early/pallas_call | solution.py:312
  150.9 3.8 %collective-permute-done.7.rest_3_ = bf16[2,128,256]{2,1,0:T(8,128)(2,1)S(1)} collective-permute-done((bf16[2,128,256]{2,1,0:T(8,128)(2,1)}, bf16[2,128,256]{2,1,0:T(8,128)(2,1)S(1)}, u32[]{:S(2)}, u32[]{:S(2)}) %collective-permute-start.7) | collective-permute-done | bytes 131104 | tf_op jit(solution)/shard_map/ppermute | solution.py:400
  154.8 3.4 %collective-permute-done.8.rest_4_ = bf16[2,128,256]{2,1,0:T(8,128)(2,1)S(1)} collective-permute-done((bf16[2,128,256]{2,1,0:T(8,128)(2,1)}, bf16[2,128,256]{2,1,0:T(8,128)(2,1)S(1)}, u32[]{:S(2)}, u32[]{:S(2)}) %collective-permute-start.8) | collective-permute-done | bytes 131104 | tf_op jit(solution)/shard_map/ppermute | solution.py:400
  158.1 4.8 %remap_last.1 = bf16[24,128,256]{2,1,0:T(8,128)(2,1)} custom-call(s32[24,35]{1,0:T(8,128)S(1)} %concatenate.3.table, bf16[24,16,128,128]{3,2,1,0:T(8,128)(2,1)} %weights.3, bf16[2,128,256]{2,1,0:T(8,128)(2,1)S(1)} %collective-permute-done.4.rest_0_, bf16[2,128,256]{2,1,0:T(8,128)(2,1)S(1)} %collective-permute-done.5.rest_1_, ...), custom_call_target="tpu_custom_call" | custom-call | flops 1610612736 | bytes 6291456 | tf_op jit(solution)/shard_map/remap_last/pallas_call | solution.py:312
  (62 shorter events, 7.5 us)
Async XLA Ops:
  1.7 25.1 %collective-permute-start.2 = (bf16[180,256]{1,0:T(8,128)(2,1)S(1)}, bf16[180,256]{1,0:T(8,128)(2,1)S(1)}, u32[]{:S(2)}, u32[]{:S(2)}) collective-permute-start(bf16[180,256]{1,0:T(8,128)(2,1)S(1)} %get-tuple-element.102), channel_id=1, source_target_pairs={{0,1},{1,0},{2,3},{3,2},{4,5},{5,4},{6,7},{7,6},{8,9},{9,8},{10,11... | collective-permute-start | bytes 276488 | tf_op jit(solution)/shard_map/ppermute | solution.py:370
  4.7 22.0 %collective-permute-start.3 = (bf16[180,256]{1,0:T(8,128)(2,1)S(1)}, bf16[180,256]{1,0:T(8,128)(2,1)S(1)}, u32[]{:S(2)}, u32[]{:S(2)}) collective-permute-start(bf16[180,256]{1,0:T(8,128)(2,1)S(1)} %get-tuple-element.101), channel_id=1, source_target_pairs={{7,31},{15,23},{23,15},{31,7},{1,2},{2,1},{9,10},{10,9},{17,18},{1... | collective-permute-start | bytes 276488 | tf_op jit(solution)/shard_map/ppermute | solution.py:376
  6.7 14.7 %all-to-all-start = ((s32[32,1,2]{2,1,0:T(1,128)}), s32[32,1,2]{2,1,0:T(1,128)S(1)}, u32[]{:S(2)}, u32[]{:S(2)}) async-start(s32[32,1,2]{2,1,0:T(1,128)} %copy.39), calls=%async_computation | async-start | bytes 32768 | tf_op jit(solution)/shard_map/all_to_all | solution.py:360
  15.2 11.6 %collective-permute-start = (bf16[64,256]{1,0:T(8,128)(2,1)S(1)}, bf16[64,256]{1,0:T(8,128)(2,1)S(1)}, u32[]{:S(2)}, u32[]{:S(2)}) collective-permute-start(bf16[64,256]{1,0:T(8,128)(2,1)S(1)} %get-tuple-element.100), channel_id=1, source_target_pairs={{8,0},{16,8},{24,16},{0,24},{9,1},{17,9},{25,17},{1,25},{10,2},{18... | collective-permute-start | bytes 98312 | tf_op jit(solution)/shard_map/ppermute | solution.py:365
  16.7 10.1 %collective-permute-start.1 = (bf16[64,256]{1,0:T(8,128)(2,1)S(1)}, bf16[64,256]{1,0:T(8,128)(2,1)S(1)}, u32[]{:S(2)}, u32[]{:S(2)}) collective-permute-start(bf16[64,256]{1,0:T(8,128)(2,1)S(1)} %get-tuple-element.99), channel_id=1, source_target_pairs={{0,8},{8,16},{16,24},{24,0},{1,9},{9,17},{17,25},{25,1},{2,10},{10... | collective-permute-start | bytes 98312 | tf_op jit(solution)/shard_map/ppermute | solution.py:364
  33.9 43.3 %copy-start.4 = (s32[24,16]{0,1:T(8,128)S(1)}, s32[24,16]{0,1:T(8,128)}, u32[]{:S(2)}) copy-start(s32[24,16]{0,1:T(8,128)} %param.9) | copy-start | bytes 4612
  33.9 43.3 %copy-start.5 = (s32[24]{0:T(128)S(1)}, s32[24]{0:T(128)}, u32[]{:S(2)}) copy-start(s32[24]{0:T(128)} %param.10) | copy-start | bytes 292
  38.1 5.8 %collective-permute-start.25 = (bf16[2,128,256]{2,1,0:T(8,128)(2,1)S(1)}, bf16[2,128,256]{2,1,0:T(8,128)(2,1)S(1)}, u32[]{:S(2)}, u32[]{:S(2)}) collective-permute-start(bf16[2,128,256]{2,1,0:T(8,128)(2,1)S(1)} %get-tuple-element.51.rest_0_), channel_id=1, source_target_pairs={{0,10},{1,11},{2,8},{3,9},{4,14},{5,15},{6,12},{7,13},{8,2},{9,3},... | collective-permute-start | bytes 393224 | tf_op jit(solution)/shard_map/ppermute | solution.py:400
  38.2 8.7 %collective-permute-start.26 = (bf16[2,128,256]{2,1,0:T(8,128)(2,1)S(1)}, bf16[2,128,256]{2,1,0:T(8,128)(2,1)S(1)}, u32[]{:S(2)}, u32[]{:S(2)}) collective-permute-start(bf16[2,128,256]{2,1,0:T(8,128)(2,1)S(1)} %get-tuple-element.81), channel_id=1, source_target_pairs={{0,11},{1,10},{2,9},{3,8},{4,15},{5,14},{6,13},{7,12},{8,3},{9,2},... | collective-permute-start | bytes 393224 | tf_op jit(solution)/shard_map/ppermute | solution.py:400
  40.0 8.3 %collective-permute-start.27 = (bf16[2,128,256]{2,1,0:T(8,128)(2,1)S(1)}, bf16[2,128,256]{2,1,0:T(8,128)(2,1)S(1)}, u32[]{:S(2)}, u32[]{:S(2)}) collective-permute-start(bf16[2,128,256]{2,1,0:T(8,128)(2,1)S(1)} %get-tuple-element.82), channel_id=1, source_target_pairs={{0,16},{1,17},{2,18},{3,19},{4,20},{5,21},{6,22},{7,23},{8,24},{9,... | collective-permute-start | bytes 393224 | tf_op jit(solution)/shard_map/ppermute | solution.py:400
  40.6 14.5 %collective-permute-start.28 = (bf16[2,128,256]{2,1,0:T(8,128)(2,1)S(1)}, bf16[2,128,256]{2,1,0:T(8,128)(2,1)S(1)}, u32[]{:S(2)}, u32[]{:S(2)}) collective-permute-start(bf16[2,128,256]{2,1,0:T(8,128)(2,1)S(1)} %get-tuple-element.83), channel_id=1, source_target_pairs={{0,17},{1,16},{2,19},{3,18},{4,21},{5,20},{6,23},{7,22},{8,25},{9,... | collective-permute-start | bytes 393224 | tf_op jit(solution)/shard_map/ppermute | solution.py:400
  42.9 12.2 %collective-permute-start.29 = (bf16[2,128,256]{2,1,0:T(8,128)(2,1)S(1)}, bf16[2,128,256]{2,1,0:T(8,128)(2,1)S(1)}, u32[]{:S(2)}, u32[]{:S(2)}) collective-permute-start(bf16[2,128,256]{2,1,0:T(8,128)(2,1)S(1)} %get-tuple-element.84), channel_id=1, source_target_pairs={{0,18},{1,19},{2,16},{3,17},{4,22},{5,23},{6,20},{7,21},{8,26},{9,... | collective-permute-start | bytes 393224 | tf_op jit(solution)/shard_map/ppermute | solution.py:400
  44.0 12.8 %collective-permute-start.30 = (bf16[2,128,256]{2,1,0:T(8,128)(2,1)S(1)}, bf16[2,128,256]{2,1,0:T(8,128)(2,1)S(1)}, u32[]{:S(2)}, u32[]{:S(2)}) collective-permute-start(bf16[2,128,256]{2,1,0:T(8,128)(2,1)S(1)} %get-tuple-element.85), channel_id=1, source_target_pairs={{0,19},{1,18},{2,17},{3,16},{4,23},{5,22},{6,21},{7,20},{8,27},{9,... | collective-permute-start | bytes 393224 | tf_op jit(solution)/shard_map/ppermute | solution.py:400
  46.9 26.5 %collective-permute-start.15 = (bf16[2,128,256]{2,1,0:T(8,128)(2,1)S(1)}, bf16[2,128,256]{2,1,0:T(8,128)(2,1)S(1)}, u32[]{:S(2)}, u32[]{:S(2)}) collective-permute-start(bf16[2,128,256]{2,1,0:T(8,128)(2,1)S(1)} %get-tuple-element.50.rest_0_), channel_id=1, source_target_pairs={{0,1},{1,0},{2,3},{3,2},{4,5},{5,4},{6,7},{7,6},{8,9},{9,8},{10,11... | collective-permute-start | bytes 393224 | tf_op jit(solution)/shard_map/ppermute | solution.py:400
  48.3 16.6 %collective-permute-start.31 = (bf16[2,128,256]{2,1,0:T(8,128)(2,1)S(1)}, bf16[2,128,256]{2,1,0:T(8,128)(2,1)S(1)}, u32[]{:S(2)}, u32[]{:S(2)}) collective-permute-start(bf16[2,128,256]{2,1,0:T(8,128)(2,1)S(1)} %get-tuple-element.86), channel_id=1, source_target_pairs={{0,24},{1,25},{2,26},{3,27},{4,28},{5,29},{6,30},{7,31},{8,16},{9,... | collective-permute-start | bytes 393224 | tf_op jit(solution)/shard_map/ppermute | solution.py:400
  55.1 13.4 %collective-permute-start.32 = (bf16[2,128,256]{2,1,0:T(8,128)(2,1)S(1)}, bf16[2,128,256]{2,1,0:T(8,128)(2,1)S(1)}, u32[]{:S(2)}, u32[]{:S(2)}) collective-permute-start(bf16[2,128,256]{2,1,0:T(8,128)(2,1)S(1)} %get-tuple-element.87), channel_id=1, source_target_pairs={{0,25},{1,24},{2,27},{3,26},{4,29},{5,28},{6,31},{7,30},{8,17},{9,... | collective-permute-start | bytes 393224 | tf_op jit(solution)/shard_map/ppermute | solution.py:400
  55.1 17.4 %collective-permute-start.33 = (bf16[2,128,256]{2,1,0:T(8,128)(2,1)S(1)}, bf16[2,128,256]{2,1,0:T(8,128)(2,1)S(1)}, u32[]{:S(2)}, u32[]{:S(2)}) collective-permute-start(bf16[2,128,256]{2,1,0:T(8,128)(2,1)S(1)} %get-tuple-element.88), channel_id=1, source_target_pairs={{0,26},{1,27},{2,24},{3,25},{4,30},{5,31},{6,28},{7,29},{8,18},{9,... | collective-permute-start | bytes 393224 | tf_op jit(solution)/shard_map/ppermute | solution.py:400
  56.7 15.7 %collective-permute-start.34 = (bf16[2,128,256]{2,1,0:T(8,128)(2,1)S(1)}, bf16[2,128,256]{2,1,0:T(8,128)(2,1)S(1)}, u32[]{:S(2)}, u32[]{:S(2)}) collective-permute-start(bf16[2,128,256]{2,1,0:T(8,128)(2,1)S(1)} %get-tuple-element.89), channel_id=1, source_target_pairs={{0,27},{1,26},{2,25},{3,24},{4,31},{5,30},{6,29},{7,28},{8,19},{9,... | collective-permute-start | bytes 393224 | tf_op jit(solution)/shard_map/ppermute | solution.py:400
  62.2 0.6 copy-start
  62.8 0.7 copy-start.1
  63.5 0.7 copy-start.2
  64.1 0.6 copy-start.3
  64.9 12.3 %collective-permute-start.16 = (bf16[2,128,256]{2,1,0:T(8,128)(2,1)S(1)}, bf16[2,128,256]{2,1,0:T(8,128)(2,1)S(1)}, u32[]{:S(2)}, u32[]{:S(2)}) collective-permute-start(bf16[2,128,256]{2,1,0:T(8,128)(2,1)S(1)} %get-tuple-element.72), channel_id=1, source_target_pairs={{0,12},{1,13},{2,14},{3,15},{4,8},{5,9},{6,10},{7,11},{8,4},{9,5},... | collective-permute-start | bytes 393224 | tf_op jit(solution)/shard_map/ppermute | solution.py:400
  68.5 11.0 %collective-permute-start.17 = (bf16[2,128,256]{2,1,0:T(8,128)(2,1)S(1)}, bf16[2,128,256]{2,1,0:T(8,128)(2,1)S(1)}, u32[]{:S(2)}, u32[]{:S(2)}) collective-permute-start(bf16[2,128,256]{2,1,0:T(8,128)(2,1)S(1)} %get-tuple-element.73), channel_id=1, source_target_pairs={{0,2},{1,3},{2,0},{3,1},{4,6},{5,7},{6,4},{7,5},{8,10},{9,11},{10,... | collective-permute-start | bytes 393224 | tf_op jit(solution)/shard_map/ppermute | solution.py:400
  72.5 10.0 %collective-permute-start.18 = (bf16[2,128,256]{2,1,0:T(8,128)(2,1)S(1)}, bf16[2,128,256]{2,1,0:T(8,128)(2,1)S(1)}, u32[]{:S(2)}, u32[]{:S(2)}) collective-permute-start(bf16[2,128,256]{2,1,0:T(8,128)(2,1)S(1)} %get-tuple-element.74), channel_id=1, source_target_pairs={{0,13},{1,12},{2,15},{3,14},{4,9},{5,8},{6,11},{7,10},{8,5},{9,4},... | collective-permute-start | bytes 393224 | tf_op jit(solution)/shard_map/ppermute | solution.py:400
  72.5 13.0 %collective-permute-start.19 = (bf16[2,128,256]{2,1,0:T(8,128)(2,1)S(1)}, bf16[2,128,256]{2,1,0:T(8,128)(2,1)S(1)}, u32[]{:S(2)}, u32[]{:S(2)}) collective-permute-start(bf16[2,128,256]{2,1,0:T(8,128)(2,1)S(1)} %get-tuple-element.75), channel_id=1, source_target_pairs={{0,3},{1,2},{2,1},{3,0},{4,7},{5,6},{6,5},{7,4},{8,11},{9,10},{10,... | collective-permute-start | bytes 393224 | tf_op jit(solution)/shard_map/ppermute | solution.py:400
  73.4 13.8 %collective-permute-start.20 = (bf16[2,128,256]{2,1,0:T(8,128)(2,1)S(1)}, bf16[2,128,256]{2,1,0:T(8,128)(2,1)S(1)}, u32[]{:S(2)}, u32[]{:S(2)}) collective-permute-start(bf16[2,128,256]{2,1,0:T(8,128)(2,1)S(1)} %get-tuple-element.76), channel_id=1, source_target_pairs={{0,14},{1,15},{2,12},{3,13},{4,10},{5,11},{6,8},{7,9},{8,6},{9,7},... | collective-permute-start | bytes 393224 | tf_op jit(solution)/shard_map/ppermute | solution.py:400
  77.3 39.4 %collective-permute-start.11 = (bf16[2,128,256]{2,1,0:T(8,128)(2,1)S(1)}, bf16[2,128,256]{2,1,0:T(8,128)(2,1)S(1)}, u32[]{:S(2)}, u32[]{:S(2)}) collective-permute-start(bf16[2,128,256]{2,1,0:T(8,128)(2,1)S(1)} %get-tuple-element.49.rest_0_), channel_id=1, source_target_pairs={{0,4},{1,5},{2,6},{3,7},{4,0},{5,1},{6,2},{7,3},{8,12},{9,13},{10,... | collective-permute-start | bytes 393224 | tf_op jit(solution)/shard_map/ppermute | solution.py:400
  79.5 16.0 %collective-permute-start.21 = (bf16[2,128,256]{2,1,0:T(8,128)(2,1)S(1)}, bf16[2,128,256]{2,1,0:T(8,128)(2,1)S(1)}, u32[]{:S(2)}, u32[]{:S(2)}) collective-permute-start(bf16[2,128,256]{2,1,0:T(8,128)(2,1)S(1)} %get-tuple-element.77), channel_id=1, source_target_pairs={{0,8},{1,9},{2,10},{3,11},{4,12},{5,13},{6,14},{7,15},{8,0},{9,1},... | collective-permute-start | bytes 393224 | tf_op jit(solution)/shard_map/ppermute | solution.py:400
  82.4 13.8 %collective-permute-start.22 = (bf16[2,128,256]{2,1,0:T(8,128)(2,1)S(1)}, bf16[2,128,256]{2,1,0:T(8,128)(2,1)S(1)}, u32[]{:S(2)}, u32[]{:S(2)}) collective-permute-start(bf16[2,128,256]{2,1,0:T(8,128)(2,1)S(1)} %get-tuple-element.78), channel_id=1, source_target_pairs={{0,15},{1,14},{2,13},{3,12},{4,11},{5,10},{6,9},{7,8},{8,7},{9,6},... | collective-permute-start | bytes 393224 | tf_op jit(solution)/shard_map/ppermute | solution.py:400
  85.5 11.8 %collective-permute-start.23 = (bf16[2,128,256]{2,1,0:T(8,128)(2,1)S(1)}, bf16[2,128,256]{2,1,0:T(8,128)(2,1)S(1)}, u32[]{:S(2)}, u32[]{:S(2)}) collective-permute-start(bf16[2,128,256]{2,1,0:T(8,128)(2,1)S(1)} %get-tuple-element.79), channel_id=1, source_target_pairs={{0,9},{1,8},{2,11},{3,10},{4,13},{5,12},{6,15},{7,14},{8,1},{9,0},... | collective-permute-start | bytes 393224 | tf_op jit(solution)/shard_map/ppermute | solution.py:400
  87.2 26.0 %collective-permute-start.24 = (bf16[2,128,256]{2,1,0:T(8,128)(2,1)S(1)}, bf16[2,128,256]{2,1,0:T(8,128)(2,1)S(1)}, u32[]{:S(2)}, u32[]{:S(2)}) collective-permute-start(bf16[2,128,256]{2,1,0:T(8,128)(2,1)S(1)} %get-tuple-element.80), channel_id=1, source_target_pairs={{0,20},{1,21},{2,22},{3,23},{4,16},{5,17},{6,18},{7,19},{8,28},{9,... | collective-permute-start | bytes 393224 | tf_op jit(solution)/shard_map/ppermute | solution.py:400
  95.5 26.7 %collective-permute-start.12 = (bf16[2,128,256]{2,1,0:T(8,128)(2,1)}, bf16[2,128,256]{2,1,0:T(8,128)(2,1)S(1)}, u32[]{:S(2)}, u32[]{:S(2)}) collective-permute-start(bf16[2,128,256]{2,1,0:T(8,128)(2,1)} %get-tuple-element.69), channel_id=1, source_target_pairs={{0,5},{1,4},{2,7},{3,6},{4,1},{5,0},{6,3},{7,2},{8,13},{9,12},{10,... | collective-permute-start | bytes 393224 | tf_op jit(solution)/shard_map/ppermute | solution.py:400
  96.2 27.9 %collective-permute-start.13 = (bf16[2,128,256]{2,1,0:T(8,128)(2,1)}, bf16[2,128,256]{2,1,0:T(8,128)(2,1)S(1)}, u32[]{:S(2)}, u32[]{:S(2)}) collective-permute-start(bf16[2,128,256]{2,1,0:T(8,128)(2,1)} %get-tuple-element.70), channel_id=1, source_target_pairs={{0,6},{1,7},{2,4},{3,5},{4,2},{5,3},{6,0},{7,1},{8,14},{9,15},{10,... | collective-permute-start | bytes 393224 | tf_op jit(solution)/shard_map/ppermute | solution.py:400
  97.3 30.0 %collective-permute-start.14 = (bf16[2,128,256]{2,1,0:T(8,128)(2,1)}, bf16[2,128,256]{2,1,0:T(8,128)(2,1)}, u32[]{:S(2)}, u32[]{:S(2)}) collective-permute-start(bf16[2,128,256]{2,1,0:T(8,128)(2,1)} %get-tuple-element.71), channel_id=1, source_target_pairs={{0,7},{1,6},{2,5},{3,4},{4,3},{5,2},{6,1},{7,0},{8,15},{9,14},{10,... | collective-permute-start | bytes 393224 | tf_op jit(solution)/shard_map/ppermute | solution.py:400
  113.2 15.7 %collective-permute-start.10 = (bf16[2,128,256]{2,1,0:T(8,128)(2,1)}, bf16[2,128,256]{2,1,0:T(8,128)(2,1)S(1)}, u32[]{:S(2)}, u32[]{:S(2)}) collective-permute-start(bf16[2,128,256]{2,1,0:T(8,128)(2,1)} %get-tuple-element.68), channel_id=1, source_target_pairs={{0,31},{1,30},{2,29},{3,28},{4,27},{5,26},{6,25},{7,24},{8,23},{9,... | collective-permute-start | bytes 393224 | tf_op jit(solution)/shard_map/ppermute | solution.py:400
  116.7 24.7 %collective-permute-start.4 = (bf16[2,128,256]{2,1,0:T(8,128)(2,1)}, bf16[2,128,256]{2,1,0:T(8,128)(2,1)S(1)}, u32[]{:S(2)}, u32[]{:S(2)}) collective-permute-start(bf16[2,128,256]{2,1,0:T(8,128)(2,1)} %get-tuple-element.62), channel_id=1, source_target_pairs={{0,21},{1,20},{2,23},{3,22},{4,17},{5,16},{6,19},{7,18},{8,29},{9,... | collective-permute-start | bytes 393224 | tf_op jit(solution)/shard_map/ppermute | solution.py:400
  122.2 28.7 %collective-permute-start.5 = (bf16[2,128,256]{2,1,0:T(8,128)(2,1)}, bf16[2,128,256]{2,1,0:T(8,128)(2,1)S(1)}, u32[]{:S(2)}, u32[]{:S(2)}) collective-permute-start(bf16[2,128,256]{2,1,0:T(8,128)(2,1)} %copy-done.3), channel_id=1, source_target_pairs={{0,22},{1,23},{2,20},{3,21},{4,18},{5,19},{6,16},{7,17},{8,30},{9,... | collective-permute-start | bytes 393224 | tf_op jit(solution)/shard_map/ppermute | solution.py:400
  124.1 26.8 %collective-permute-start.6 = (bf16[2,128,256]{2,1,0:T(8,128)(2,1)}, bf16[2,128,256]{2,1,0:T(8,128)(2,1)S(1)}, u32[]{:S(2)}, u32[]{:S(2)}) collective-permute-start(bf16[2,128,256]{2,1,0:T(8,128)(2,1)} %copy-done.2), channel_id=1, source_target_pairs={{0,23},{1,22},{2,21},{3,20},{4,19},{5,18},{6,17},{7,16},{8,31},{9,... | collective-permute-start | bytes 393224 | tf_op jit(solution)/shard_map/ppermute | solution.py:400
  127.3 27.5 %collective-permute-start.7 = (bf16[2,128,256]{2,1,0:T(8,128)(2,1)}, bf16[2,128,256]{2,1,0:T(8,128)(2,1)S(1)}, u32[]{:S(2)}, u32[]{:S(2)}) collective-permute-start(bf16[2,128,256]{2,1,0:T(8,128)(2,1)} %copy-done.1), channel_id=1, source_target_pairs={{0,28},{1,29},{2,30},{3,31},{4,24},{5,25},{6,26},{7,27},{8,20},{9,... | collective-permute-start | bytes 393224 | tf_op jit(solution)/shard_map/ppermute | solution.py:400
  128.9 29.3 %collective-permute-start.8 = (bf16[2,128,256]{2,1,0:T(8,128)(2,1)}, bf16[2,128,256]{2,1,0:T(8,128)(2,1)S(1)}, u32[]{:S(2)}, u32[]{:S(2)}) collective-permute-start(bf16[2,128,256]{2,1,0:T(8,128)(2,1)} %copy-done), channel_id=1, source_target_pairs={{0,29},{1,28},{2,31},{3,30},{4,25},{5,24},{6,27},{7,26},{8,21},{9,... | collective-permute-start | bytes 393224 | tf_op jit(solution)/shard_map/ppermute | solution.py:400
  141.4 16.8 %collective-permute-start.9 = (bf16[2,128,256]{2,1,0:T(8,128)(2,1)S(1)}, bf16[2,128,256]{2,1,0:T(8,128)(2,1)S(1)}, u32[]{:S(2)}, u32[]{:S(2)}) collective-permute-start(bf16[2,128,256]{2,1,0:T(8,128)(2,1)S(1)} %get-tuple-element.67), channel_id=1, source_target_pairs={{0,30},{1,31},{2,28},{3,29},{4,26},{5,27},{6,24},{7,25},{8,22},{9,... | collective-permute-start | bytes 393224 | tf_op jit(solution)/shard_map/ppermute | solution.py:400
where the time goes:
time: 164 us; the launch traced here: 163 us
  starting transfers between devices  79.5 us (48%)
  waiting for transfers between devices  37.5 us (23%)
  Pallas kernels  31.9 us (19%)
  local copies, waits for them, and re-layouts  12.8 us (8%)
    ppermute x31, starting transfers between devices, body(): arrived[m] = lax.ppermute(blocks, AXES, pairs) if m else blocks  66.7 us
    ppermute x31, waiting for transfers between devices, body(): arrived[m] = lax.ppermute(blocks, AXES, pairs) if m else blocks  33.8 us
    pallas_call x4, Pallas kernels, smooth_blocks(): pl.pallas_call(functools.partial(smooth_kernel, masks, columns, rows, cap...  15.5 us
    pallas_call x2, Pallas kernels, remap(): pl.pallas_call(functools.partial(remap_kernel, masks, cap, slots, last, c...  11.2 us
    all_to_all x1, starting transfers between devices, body(): lax.all_to_all(requests[0], AXES, split_axis=0, concat_axis=0, tiled=True)  7.63 us
    pallas_call x1, Pallas kernels, flatten_cells(): pl.pallas_call(flatten_kernel, out_shape=jax.ShapeDtypeStruct((pieces * c...  5.26 us
    all_to_all x1, waiting for transfers between devices, body(): lax.all_to_all(requests[0], AXES, split_axis=0, concat_axis=0, tiled=True)  3.74 us
  transfers between devices with their start and end apart: 36, of which 10 were waited for; matrix products, arithmetic and copies ran while one was open for 6% of the time, Pallas kernels for 10%

commit v1 on v0

--- a/solution.py
+++ b/solution.py
@@ -202,8 +202,9 @@
     blocks, held, weight_sem, *made = rest
     dests, terms = held.shape[:2]
     me = table[0, table.shape[1] - 1]
-    first = min(4, terms)
-    bounds = [n for n in (8,) if n < terms] + [terms]
+    stock = min(4, terms)
+    first = min(2, terms) if last else stock
+    bounds = [n for n in ((4, 8) if last else (8,)) if n < terms] + [terms]
 
     def number(dest):
         return table[dest, column + terms]
@@ -220,13 +221,15 @@
         term = table[dest, column + place] >> 16
         return pltpu.make_async_copy(weights.at[dest, term], held.at[dest, place], weight_sem.at[dest])
 
-    begin = first if last else 0
-
-    @pl.loop(0, dests)
-    def _(dest):
-        @pl.loop(begin, used(dest))
-        def _(place):
-            weight_copy(dest, place).start()
+    begin = stock if last else 0
+
+    @pl.when(table[0, table.shape[1] - 2] > begin if last else table[0, table.shape[1] - 2] >= 0)
+    def _():
+        @pl.loop(0, dests)
+        def _(dest):
+            @pl.loop(begin, used(dest))
+            def _(place):
+                weight_copy(dest, place).start()
 
     def later_copy(dest, place):
         term = table[dest, column + terms + 1 + place] >> 16
@@ -236,7 +239,7 @@
 
         @pl.loop(0, dests)
         def _(dest):
-            for place in range(first):
+            for place in range(stock):
                 later_copy(dest, place).start()
 
     blocks[slots] = jnp.zeros(blocks.shape[1:], blocks.dtype)
@@ -245,7 +248,7 @@
             blocks[(me ^ mask) * cap + c] = ref[c]
 
     def product(dest, low, high):
-        left = [ready[dest, g] if last and g < first else held[dest, g] for g in range(low, high)]
+        left = [ready[dest, g] if last and g < stock else held[dest, g] for g in range(low, high)]
         right = [blocks[table[dest, column + g] & 65535] for g in range(low, high)]
         return jnp.dot(
             jnp.concatenate(left, 1), jnp.concatenate(right, 0), preferred_element_type=jnp.float32
@@ -264,29 +267,44 @@
 
     @pl.loop(0, dests // together)
     def _(group):
-        for u in range(together):
-
-            @pl.loop(begin, used(group * together + u))
-            def _(place):
-                weight_copy(group * together + u, place).wait()
-
+        def wait():
+            for u in range(together):
+
+                @pl.loop(begin, used(group * together + u))
+                def _(place):
+                    weight_copy(group * together + u, place).wait()
+
+        def more():
+            for u in range(together):
+                dest = group * together + u
+                low = first
+                for bound in bounds:
+
+                    @pl.when((number(dest) > low) & (number(dest) <= bound) if last else number(dest) > low)
+                    def _():
+                        if last:
+                            store(dest, start_ref[dest] + product(dest, 0, bound))
+                        else:
+                            store(dest, out_ref[dest] + product(dest, low, bound))
+
+                    low = bound
+
+        if not last:
+            wait()
         for u in range(together):
             dest = group * together + u
             value = product(dest, 0, first)
             store(dest, start_ref[dest] + value if last else value)
-        for u in range(together):
-            dest = group * together + u
-            low = first
-            for bound in bounds:
-
-                @pl.when((number(dest) > low) & (number(dest) <= bound) if last else number(dest) > low)
-                def _():
-                    if last:
-                        store(dest, start_ref[dest] + product(dest, 0, bound))
-                    else:
-                        store(dest, out_ref[dest] + product(dest, low, bound))
-
-                low = bound
+        most = number(group * together)
+        for u in range(1, together):
+            most = jnp.maximum(most, number(group * together + u))
+
+        @pl.when(most > first)
+        def _():
+            if last:
+                wait()
+            more()
+
         if last:
             for u in range(together):
                 send(group * together + u).start()
@@ -296,7 +314,7 @@
         if last:
             send(dest).wait()
         else:
-            for place in range(first):
+            for place in range(stock):
                 later_copy(dest, place).wait()
 
 
@@ -382,13 +400,14 @@
     half = n_oy // 2
     across = [m for m in range(devices) if m & half]
     beside = [m for m in range(devices) if not m & half]
-    lead = 4
+    lead = min(3, len(across))
     order = across[:lead]
     for i, m in enumerate(beside[1:] + [beside[0]]):
         order += [m] + across[lead + i : lead + i + 1]
     late = across[-max(1, min(7, len(across) * 7 // 16)) :]
     order = [m for m in order if m not in late] + late
-    groups = [order[:lead]] + [order[i : i + 10] for i in range(lead, devices, 10)]
+    groups = [order[:lead], order[lead : lead + 8]]
+    groups += [order[i : i + 10] for i in range(lead + 8, devices, 10)]
     arrived, before = {}, []
     for number, group in enumerate(groups):
         made = smooth_blocks(tuple(group), asked, place, cells, coeff, east, west, inner, outer, before)
@@ -405,7 +424,8 @@
     is_late = functools.reduce(jnp.logical_or, [offset == m for m in late])
     early = [m for m in order if m not in late]
     parts = term_table(slot_ids, live & ~is_late, slots) + term_table(slot_ids, live & is_late, slots)
-    table = jnp.concatenate(parts + [jnp.full_like(parts[1], me)], axis=1)
+    most = jnp.full_like(parts[1], jnp.max(parts[3]))
+    table = jnp.concatenate(parts + [most, jnp.full_like(parts[1], me)], axis=1)
     partial = remap(tuple(early), cap, slots, 0, table, remap_weights, [arrived[m] for m in early], None, jnp.float32)
     return remap(
         tuple(late), cap, slots, term_total + 1, table, remap_weights, [arrived[m] for m in late], partial, jnp.bfloat16

time: 164 us -> 165 us (level)
  the two profiles are of different devices: /device:TPU:0 before, /device:TPU:24 now
where the time goes in v1:
time: 165 us
  starting transfers between devices  74.9 us (45%)
  Pallas kernels  46.3 us (28%)
  waiting for transfers between devices  27.2 us (16%)
  local copies, waits for them, and re-layouts  14 us (8%)
  other arithmetic  2.25 us (1%)
    ppermute x31, starting transfers between devices, body(): arrived[m] = lax.ppermute(blocks, AXES, pairs) if m else blocks  63.8 us
    ppermute x31, waiting for transfers between devices, body(): arrived[m] = lax.ppermute(blocks, AXES, pairs) if m else blocks  26.3 us
    pallas_call x2, Pallas kernels, remap(): pl.pallas_call(functools.partial(remap_kernel, masks, cap, slots, last, c...  24.1 us
    pallas_call x5, Pallas kernels, smooth_blocks(): pl.pallas_call(functools.partial(smooth_kernel, masks, columns, rows, cap...  16.9 us
    all_to_all x1, starting transfers between devices, body(): lax.all_to_all(requests[0], AXES, split_axis=0, concat_axis=0, tiled=True)  5.98 us
    pallas_call x1, Pallas kernels, flatten_cells(): pl.pallas_call(flatten_kernel, out_shape=jax.ShapeDtypeStruct((pieces * c...  5.26 us
  transfers between devices with their start and end apart: 36, of which 10 were waited for; matrix products, arithmetic and copies ran while one was open for 7% of the time, Pallas kernels for 14%

profile of v1, /device:TPU:24, one launch (start us, length us, event | category | flops | bytes accessed | tf_op | source)
XLA Modules:
  0.0 164.9 jit_solution(17555329616895594518)
XLA Ops:
  0.0 1.6 fusion.5
  1.7 1.6 collective-permute-start.2
  3.2 2.3 %collective-permute-start.3 = (bf16[180,256]{1,0:T(8,128)(2,1)S(1)}, bf16[180,256]{1,0:T(8,128)(2,1)S(1)}, u32[]{:S(2)}, u32[]{:S(2)}) collective-permute-start(bf16[180,256]{1,0:T(8,128)(2,1)S(1)} %get-tuple-element.85), channel_id=1, source_target_pairs={{7,31},{15,23},{23,15},{31,7},{1,2},{2,1},{9,10},{10,9},{17,18},{1... | collective-permute-start | bytes 276488 | tf_op jit(solution)/shard_map/ppermute | solution.py:394
  5.6 1.4 copy.41
  6.9 6.0 %all-to-all-start = ((s32[32,1,2]{2,1,0:T(1,128)}), s32[32,1,2]{2,1,0:T(1,128)S(1)}, u32[]{:S(2)}, u32[]{:S(2)}) async-start(s32[32,1,2]{2,1,0:T(1,128)} %copy.41), calls=%async_computation | async-start | bytes 32768 | tf_op jit(solution)/shard_map/all_to_all | solution.py:378
  13.7 1.2 collective-permute-start
  15.0 1.0 reshape.29.rest_0_.coeff_ref
  16.0 0.9 all-to-all-done
  16.9 5.3 %flatten.1.cells = bf16[744,16,256]{2,1,0:T(8,128)(2,1)S(1)} custom-call(bf16[180,64,256]{2,1,0:T(8,128)(2,1)} %bitcast.23, f32[90,128]{1,0:T(8,128)S(1)} %reshape.29.rest_0_.coeff_ref, s32[32,2]{1,0:T(8,128)S(1)} %bitcast.16), custom_call_target="tpu_custom_call" | custom-call | bytes 25165824 | tf_op jit(solution)/shard_map/flatten/pallas_call | solution.py:58
  22.2 2.6 %smooth.5 = (bf16[2,128,256]{2,1,0:T(8,128)(2,1)}, bf16[2,128,256]{2,1,0:T(8,128)(2,1)}, bf16[2,128,256]{2,1,0:T(8,128)(2,1)}) custom-call(s32[32,2]{1,0:T(8,128)S(1)} %bitcast.17, s32[3]{0:T(128)S(1)} %pad_add_fusion.place, bf16[744,16,256]{2,1,0:T(8,128)(2,1)S(1)} %flatten.1.cells, f32[90,128]{1,0:T(8,128)S(1)} %reshape.29.rest_0_.coeff_ref, ...), custom_call_target="tpu_custom_call" | custom-call | flops 1572864 | bytes 1966080 | tf_op jit(solution)/shard_map/smooth/pallas_call | solution.py:172
  24.8 3.5 %smooth.6 = (bf16[2,128,256]{2,1,0:T(8,128)(2,1)S(1)}, bf16[2,128,256]{2,1,0:T(8,128)(2,1)S(1)}, bf16[2,128,256]{2,1,0:T(8,128)(2,1)S(1)}, bf16[2,128,256]{2,1,0...) custom-call(s32[32,2]{1,0:T(8,128)S(1)} %bitcast.18, ...), custom_call_target="tpu_custom_call" | custom-call | flops 4194304 | bytes 5242880 | tf_op jit(solution)/shard_map/smooth/pallas_call | solution.py:172
  28.3 4.2 %smooth.7 = (bf16[2,128,256]{2,1,0:T(8,128)(2,1)S(1)}, bf16[2,128,256]{2,1,0:T(8,128)(2,1)S(1)}, bf16[2,128,256]{2,1,0:T(8,128)(2,1)S(1)}, bf16[2,128,256]{2,1,0...) custom-call(s32[32,2]{1,0:T(8,128)S(1)} %bitcast.19, ...), custom_call_target="tpu_custom_call" | custom-call | flops 5242880 | bytes 6553600 | tf_op jit(solution)/shard_map/smooth/pallas_call | solution.py:172
  32.5 4.8 %smooth.8 = (bf16[2,128,256]{2,1,0:T(8,128)(2,1)S(1)}, bf16[2,128,256]{2,1,0:T(8,128)(2,1)S(1)}, bf16[2,128,256]{2,1,0:T(8,128)(2,1)S(1)}, bf16[2,128,256]{2,1,0...) custom-call(s32[32,2]{1,0:T(8,128)S(1)} %bitcast.20, ...), custom_call_target="tpu_custom_call" | custom-call | flops 5242880 | bytes 6553600 | tf_op jit(solution)/shard_map/smooth/pallas_call | solution.py:172
  39.9 6.1 %collective-permute-start.32 = (bf16[2,128,256]{2,1,0:T(8,128)(2,1)S(1)}, bf16[2,128,256]{2,1,0:T(8,128)(2,1)S(1)}, u32[]{:S(2)}, u32[]{:S(2)}) collective-permute-start(bf16[2,128,256]{2,1,0:T(8,128)(2,1)S(1)} %get-tuple-element.44.rest_0_), channel_id=1, source_target_pairs={{0,25},{1,24},{2,27},{3,26},{4,29},{5,28},{6,31},{7,30},{8,17},{9,... | collective-permute-start | bytes 393224 | tf_op jit(solution)/shard_map/ppermute | solution.py:419
  46.0 1.0 collective-permute-start.34
  47.0 1.9 %collective-permute-start.22 = (bf16[2,128,256]{2,1,0:T(8,128)(2,1)S(1)}, bf16[2,128,256]{2,1,0:T(8,128)(2,1)S(1)}, u32[]{:S(2)}, u32[]{:S(2)}) collective-permute-start(bf16[2,128,256]{2,1,0:T(8,128)(2,1)S(1)} %get-tuple-element.43.rest_0_), channel_id=1, source_target_pairs={{0,9},{1,8},{2,11},{3,10},{4,13},{5,12},{6,15},{7,14},{8,1},{9,0},... | collective-permute-start | bytes 393224 | tf_op jit(solution)/shard_map/ppermute | solution.py:419
  48.9 1.3 collective-permute-done.32.rest_21_
  50.2 2.7 %collective-permute-done.33.rest_22_ = bf16[2,128,256]{2,1,0:T(8,128)(2,1)S(1)} collective-permute-done((bf16[2,128,256]{2,1,0:T(8,128)(2,1)S(1)}, bf16[2,128,256]{2,1,0:T(8,128)(2,1)S(1)}, u32[]{:S(2)}, u32[]{:S(2)}) %collective-permute-start.33) | collective-permute-done | bytes 131104 | tf_op jit(solution)/shard_map/ppermute | solution.py:419
  54.3 1.9 %collective-permute-start.26 = (bf16[2,128,256]{2,1,0:T(8,128)(2,1)S(1)}, bf16[2,128,256]{2,1,0:T(8,128)(2,1)S(1)}, u32[]{:S(2)}, u32[]{:S(2)}) collective-permute-start(bf16[2,128,256]{2,1,0:T(8,128)(2,1)S(1)} %get-tuple-element.66), channel_id=1, source_target_pairs={{0,11},{1,10},{2,9},{3,8},{4,15},{5,14},{6,13},{7,12},{8,3},{9,2},... | collective-permute-start | bytes 393224 | tf_op jit(solution)/shard_map/ppermute | solution.py:419
  56.3 1.8 %collective-permute-done.22.rest_11_ = bf16[2,128,256]{2,1,0:T(8,128)(2,1)S(1)} collective-permute-done((bf16[2,128,256]{2,1,0:T(8,128)(2,1)S(1)}, bf16[2,128,256]{2,1,0:T(8,128)(2,1)S(1)}, u32[]{:S(2)}, u32[]{:S(2)}) %collective-permute-start.22) | collective-permute-done | bytes 131104 | tf_op jit(solution)/shard_map/ppermute | solution.py:419
  58.0 2.8 %collective-permute-start.27 = (bf16[2,128,256]{2,1,0:T(8,128)(2,1)S(1)}, bf16[2,128,256]{2,1,0:T(8,128)(2,1)S(1)}, u32[]{:S(2)}, u32[]{:S(2)}) collective-permute-start(bf16[2,128,256]{2,1,0:T(8,128)(2,1)S(1)} %get-tuple-element.67), channel_id=1, source_target_pairs={{0,16},{1,17},{2,18},{3,19},{4,20},{5,21},{6,22},{7,23},{8,24},{9,... | collective-permute-start | bytes 393224 | tf_op jit(solution)/shard_map/ppermute | solution.py:419
  60.9 2.7 %collective-permute-start.28 = (bf16[2,128,256]{2,1,0:T(8,128)(2,1)S(1)}, bf16[2,128,256]{2,1,0:T(8,128)(2,1)S(1)}, u32[]{:S(2)}, u32[]{:S(2)}) collective-permute-start(bf16[2,128,256]{2,1,0:T(8,128)(2,1)S(1)} %get-tuple-element.68), channel_id=1, source_target_pairs={{0,17},{1,16},{2,19},{3,18},{4,21},{5,20},{6,23},{7,22},{8,25},{9,... | collective-permute-start | bytes 393224 | tf_op jit(solution)/shard_map/ppermute | solution.py:419
  63.6 1.1 collective-permute-start.29
  64.7 1.8 %smooth.9 = bf16[2,128,256]{2,1,0:T(8,128)(2,1)} custom-call(s32[32,2]{1,0:T(8,128)S(1)} %bitcast.21, s32[3]{0:T(128)S(1)} %pad_add_fusion.place, bf16[744,16,256]{2,1,0:T(8,128)(2,1)S(1)} %flatten.1.cells, f32[90,128]{1,0:T(8,128)S(1)} %reshape.29.rest_0_.coeff_ref, bf16[64,256]{1,0:T(8,128)(2,1)S(1)} %collective-permute-done.east_ref, ...), custom_call_target="tpu_custom_call" | custom-call | flops 524288 | bytes 655360 | tf_op jit(solution)/shard_map/smooth/pallas_call | solution.py:172
  66.5 4.4 %collective-permute-start.14 = (bf16[2,128,256]{2,1,0:T(8,128)(2,1)S(1)}, bf16[2,128,256]{2,1,0:T(8,128)(2,1)S(1)}, u32[]{:S(2)}, u32[]{:S(2)}) collective-permute-start(bf16[2,128,256]{2,1,0:T(8,128)(2,1)S(1)} %get-tuple-element.42.rest_0_), channel_id=1, source_target_pairs={{0,1},{1,0},{2,3},{3,2},{4,5},{5,4},{6,7},{7,6},{8,9},{9,8},{10,11... | collective-permute-start | bytes 393224 | tf_op jit(solution)/shard_map/ppermute | solution.py:419
  71.3 1.8 %collective-permute-start.15 = (bf16[2,128,256]{2,1,0:T(8,128)(2,1)S(1)}, bf16[2,128,256]{2,1,0:T(8,128)(2,1)S(1)}, u32[]{:S(2)}, u32[]{:S(2)}) collective-permute-start(bf16[2,128,256]{2,1,0:T(8,128)(2,1)S(1)} %get-tuple-element.56), channel_id=1, source_target_pairs={{0,7},{1,6},{2,5},{3,4},{4,3},{5,2},{6,1},{7,0},{8,15},{9,14},{10,... | collective-permute-start | bytes 393224 | tf_op jit(solution)/shard_map/ppermute | solution.py:419
  73.1 4.6 %collective-permute-start.16 = (bf16[2,128,256]{2,1,0:T(8,128)(2,1)S(1)}, bf16[2,128,256]{2,1,0:T(8,128)(2,1)S(1)}, u32[]{:S(2)}, u32[]{:S(2)}) collective-permute-start(bf16[2,128,256]{2,1,0:T(8,128)(2,1)S(1)} %get-tuple-element.57), channel_id=1, source_target_pairs={{0,2},{1,3},{2,0},{3,1},{4,6},{5,7},{6,4},{7,5},{8,10},{9,11},{10,... | collective-permute-start | bytes 393224 | tf_op jit(solution)/shard_map/ppermute | solution.py:419
  78.7 3.4 %collective-permute-start.18 = (bf16[2,128,256]{2,1,0:T(8,128)(2,1)S(1)}, bf16[2,128,256]{2,1,0:T(8,128)(2,1)S(1)}, u32[]{:S(2)}, u32[]{:S(2)}) collective-permute-start(bf16[2,128,256]{2,1,0:T(8,128)(2,1)S(1)} %get-tuple-element.59), channel_id=1, source_target_pairs={{0,3},{1,2},{2,1},{3,0},{4,7},{5,6},{6,5},{7,4},{8,11},{9,10},{10,... | collective-permute-start | bytes 393224 | tf_op jit(solution)/shard_map/ppermute | solution.py:419
  82.2 1.1 collective-permute-start.20
  83.3 4.1 %collective-permute-done.16.rest_5_ = bf16[2,128,256]{2,1,0:T(8,128)(2,1)S(1)} collective-permute-done((bf16[2,128,256]{2,1,0:T(8,128)(2,1)S(1)}, bf16[2,128,256]{2,1,0:T(8,128)(2,1)S(1)}, u32[]{:S(2)}, u32[]{:S(2)}) %collective-permute-start.16) | collective-permute-done | bytes 131104 | tf_op jit(solution)/shard_map/ppermute | solution.py:419
  88.0 1.3 collective-permute-start.11
  89.3 4.7 %collective-permute-start.12 = (bf16[2,128,256]{2,1,0:T(8,128)(2,1)}, bf16[2,128,256]{2,1,0:T(8,128)(2,1)S(1)}, u32[]{:S(2)}, u32[]{:S(2)}) collective-permute-start(bf16[2,128,256]{2,1,0:T(8,128)(2,1)} %get-tuple-element.54), channel_id=1, source_target_pairs={{0,5},{1,4},{2,7},{3,6},{4,1},{5,0},{6,3},{7,2},{8,13},{9,12},{10,... | collective-permute-start | bytes 393224 | tf_op jit(solution)/shard_map/ppermute | solution.py:419
  94.0 10.1 %collective-permute-done.19.rest_8_ = bf16[2,128,256]{2,1,0:T(8,128)(2,1)S(1)} collective-permute-done((bf16[2,128,256]{2,1,0:T(8,128)(2,1)S(1)}, bf16[2,128,256]{2,1,0:T(8,128)(2,1)S(1)}, u32[]{:S(2)}, u32[]{:S(2)}) %collective-permute-start.19) | collective-permute-done | bytes 131104 | tf_op jit(solution)/shard_map/ppermute | solution.py:419
  104.1 1.1 collective-permute-start.13
  105.4 4.4 %collective-permute-start.4 = (bf16[2,128,256]{2,1,0:T(8,128)(2,1)}, bf16[2,128,256]{2,1,0:T(8,128)(2,1)S(1)}, u32[]{:S(2)}, u32[]{:S(2)}) collective-permute-start(bf16[2,128,256]{2,1,0:T(8,128)(2,1)} %get-tuple-element.47), channel_id=1, source_target_pairs={{0,21},{1,20},{2,23},{3,22},{4,17},{5,16},{6,19},{7,18},{8,29},{9,... | collective-permute-start | bytes 393224 | tf_op jit(solution)/shard_map/ppermute | solution.py:419
  111.2 1.3 copy.52
  112.5 1.3 reduce_max.9
  113.8 1.4 copy.54
  115.2 1.2 broadcast_in_dim.82
  117.8 1.0 collective-permute-start.5
  118.8 1.9 %collective-permute-done.12.rest_1_ = bf16[2,128,256]{2,1,0:T(8,128)(2,1)S(1)} collective-permute-done((bf16[2,128,256]{2,1,0:T(8,128)(2,1)}, bf16[2,128,256]{2,1,0:T(8,128)(2,1)S(1)}, u32[]{:S(2)}, u32[]{:S(2)}) %collective-permute-start.12) | collective-permute-done | bytes 131104 | tf_op jit(solution)/shard_map/ppermute | solution.py:419
  120.7 1.9 %collective-permute-start.6 = (bf16[2,128,256]{2,1,0:T(8,128)(2,1)}, bf16[2,128,256]{2,1,0:T(8,128)(2,1)S(1)}, u32[]{:S(2)}, u32[]{:S(2)}) collective-permute-start(bf16[2,128,256]{2,1,0:T(8,128)(2,1)} %copy-done.2), channel_id=1, source_target_pairs={{0,23},{1,22},{2,21},{3,20},{4,19},{5,18},{6,17},{7,16},{8,31},{9,... | collective-permute-start | bytes 393224 | tf_op jit(solution)/shard_map/ppermute | solution.py:419
  122.6 8.2 %collective-permute-start.7 = (bf16[2,128,256]{2,1,0:T(8,128)(2,1)}, bf16[2,128,256]{2,1,0:T(8,128)(2,1)S(1)}, u32[]{:S(2)}, u32[]{:S(2)}) collective-permute-start(bf16[2,128,256]{2,1,0:T(8,128)(2,1)} %copy-done.1), channel_id=1, source_target_pairs={{0,28},{1,29},{2,30},{3,31},{4,24},{5,25},{6,26},{7,27},{8,20},{9,... | collective-permute-start | bytes 393224 | tf_op jit(solution)/shard_map/ppermute | solution.py:419
  130.9 3.9 %collective-permute-start.8 = (bf16[2,128,256]{2,1,0:T(8,128)(2,1)}, bf16[2,128,256]{2,1,0:T(8,128)(2,1)S(1)}, u32[]{:S(2)}, u32[]{:S(2)}) collective-permute-start(bf16[2,128,256]{2,1,0:T(8,128)(2,1)} %copy-done), channel_id=1, source_target_pairs={{0,29},{1,28},{2,31},{3,30},{4,25},{5,24},{6,27},{7,26},{8,21},{9,... | collective-permute-start | bytes 393224 | tf_op jit(solution)/shard_map/ppermute | solution.py:419
  134.7 3.7 %collective-permute-done.4.rest_0_ = bf16[2,128,256]{2,1,0:T(8,128)(2,1)S(1)} collective-permute-done((bf16[2,128,256]{2,1,0:T(8,128)(2,1)}, bf16[2,128,256]{2,1,0:T(8,128)(2,1)S(1)}, u32[]{:S(2)}, u32[]{:S(2)}) %collective-permute-start.4) | collective-permute-done | bytes 131104 | tf_op jit(solution)/shard_map/ppermute | solution.py:419
  138.4 2.2 %collective-permute-start.9 = (bf16[2,128,256]{2,1,0:T(8,128)(2,1)S(1)}, bf16[2,128,256]{2,1,0:T(8,128)(2,1)S(1)}, u32[]{:S(2)}, u32[]{:S(2)}) collective-permute-start(bf16[2,128,256]{2,1,0:T(8,128)(2,1)S(1)} %get-tuple-element.52), channel_id=1, source_target_pairs={{0,30},{1,31},{2,28},{3,29},{4,26},{5,27},{6,24},{7,25},{8,22},{9,... | collective-permute-start | bytes 393224 | tf_op jit(solution)/shard_map/ppermute | solution.py:419
  140.7 16.6 %remap_early.1 = (f32[24,128,256]{2,1,0:T(8,128)S(1)}, bf16[24,4,128,128]{3,2,1,0:T(8,128)(2,1)S(1)}) custom-call(s32[24,36]{1,0:T(8,128)S(1)} %concatenate.3.table, bf16[24,16,128,128]{3,2,1,0:T(8,128)(2,1)} %weights.3, bf16[2,128,256]{2,1,0:T(8,128)(2,1)S(1)} %collective-permute-done.11.rest_0_, bf16[2,128,256]{2,1,0:T(8,128)(2,1)S(1)} %collective-permute-done.12.rest_1_, ...), custom_call_target="tpu_custom_call" | custom-call | flops 1610612736 | bytes 6291456 | tf_op jit(solution)/shard_map/remap_early/pallas_call | solution.py:330
  157.4 7.5 %remap_last.1 = bf16[24,128,256]{2,1,0:T(8,128)(2,1)} custom-call(s32[24,36]{1,0:T(8,128)S(1)} %concatenate.3.table, bf16[24,16,128,128]{3,2,1,0:T(8,128)(2,1)} %weights.3, bf16[2,128,256]{2,1,0:T(8,128)(2,1)S(1)} %collective-permute-done.4.rest_0_, bf16[2,128,256]{2,1,0:T(8,128)(2,1)S(1)} %collective-permute-done.5.rest_1_, ...), custom_call_target="tpu_custom_call" | custom-call | flops 1610612736 | bytes 6291456 | tf_op jit(solution)/shard_map/remap_last/pallas_call | solution.py:330
  (65 shorter events, 10.1 us)
Async XLA Ops:
  1.7 20.5 %collective-permute-start.2 = (bf16[180,256]{1,0:T(8,128)(2,1)S(1)}, bf16[180,256]{1,0:T(8,128)(2,1)S(1)}, u32[]{:S(2)}, u32[]{:S(2)}) collective-permute-start(bf16[180,256]{1,0:T(8,128)(2,1)S(1)} %get-tuple-element.86), channel_id=1, source_target_pairs={{0,1},{1,0},{2,3},{3,2},{4,5},{5,4},{6,7},{7,6},{8,9},{9,8},{10,11... | collective-permute-start | bytes 276488 | tf_op jit(solution)/shard_map/ppermute | solution.py:388
  3.2 19.0 %collective-permute-start.3 = (bf16[180,256]{1,0:T(8,128)(2,1)S(1)}, bf16[180,256]{1,0:T(8,128)(2,1)S(1)}, u32[]{:S(2)}, u32[]{:S(2)}) collective-permute-start(bf16[180,256]{1,0:T(8,128)(2,1)S(1)} %get-tuple-element.85), channel_id=1, source_target_pairs={{7,31},{15,23},{23,15},{31,7},{1,2},{2,1},{9,10},{10,9},{17,18},{1... | collective-permute-start | bytes 276488 | tf_op jit(solution)/shard_map/ppermute | solution.py:394
  6.9 10.0 %all-to-all-start = ((s32[32,1,2]{2,1,0:T(1,128)}), s32[32,1,2]{2,1,0:T(1,128)S(1)}, u32[]{:S(2)}, u32[]{:S(2)}) async-start(s32[32,1,2]{2,1,0:T(1,128)} %copy.41), calls=%async_computation | async-start | bytes 32768 | tf_op jit(solution)/shard_map/all_to_all | solution.py:378
  13.7 8.5 %collective-permute-start = (bf16[64,256]{1,0:T(8,128)(2,1)S(1)}, bf16[64,256]{1,0:T(8,128)(2,1)S(1)}, u32[]{:S(2)}, u32[]{:S(2)}) collective-permute-start(bf16[64,256]{1,0:T(8,128)(2,1)S(1)} %get-tuple-element.84), channel_id=1, source_target_pairs={{8,0},{16,8},{24,16},{0,24},{9,1},{17,9},{25,17},{1,25},{10,2},{18... | collective-permute-start | bytes 98312 | tf_op jit(solution)/shard_map/ppermute | solution.py:383
  14.9 7.3 %collective-permute-start.1 = (bf16[64,256]{1,0:T(8,128)(2,1)S(1)}, bf16[64,256]{1,0:T(8,128)(2,1)S(1)}, u32[]{:S(2)}, u32[]{:S(2)}) collective-permute-start(bf16[64,256]{1,0:T(8,128)(2,1)S(1)} %get-tuple-element.83), channel_id=1, source_target_pairs={{0,8},{8,16},{16,24},{24,0},{1,9},{9,17},{17,25},{25,1},{2,10},{10... | collective-permute-start | bytes 98312 | tf_op jit(solution)/shard_map/ppermute | solution.py:382
  32.5 45.2 %copy-start.4 = (s32[24,16]{0,1:T(8,128)S(1)}, s32[24,16]{0,1:T(8,128)}, u32[]{:S(2)}) copy-start(s32[24,16]{0,1:T(8,128)} %param.9) | copy-start | bytes 4612
  32.5 45.2 %copy-start.5 = (s32[24]{0:T(128)S(1)}, s32[24]{0:T(128)}, u32[]{:S(2)}) copy-start(s32[24]{0:T(128)} %param.10) | copy-start | bytes 292
  37.3 0.7 copy-start
  38.0 0.6 copy-start.1
  38.6 0.7 copy-start.2
  39.3 0.7 copy-start.3
  39.9 10.2 %collective-permute-start.32 = (bf16[2,128,256]{2,1,0:T(8,128)(2,1)S(1)}, bf16[2,128,256]{2,1,0:T(8,128)(2,1)S(1)}, u32[]{:S(2)}, u32[]{:S(2)}) collective-permute-start(bf16[2,128,256]{2,1,0:T(8,128)(2,1)S(1)} %get-tuple-element.44.rest_0_), channel_id=1, source_target_pairs={{0,25},{1,24},{2,27},{3,26},{4,29},{5,28},{6,31},{7,30},{8,17},{9,... | collective-permute-start | bytes 393224 | tf_op jit(solution)/shard_map/ppermute | solution.py:419
  46.0 6.9 %collective-permute-start.33 = (bf16[2,128,256]{2,1,0:T(8,128)(2,1)S(1)}, bf16[2,128,256]{2,1,0:T(8,128)(2,1)S(1)}, u32[]{:S(2)}, u32[]{:S(2)}) collective-permute-start(bf16[2,128,256]{2,1,0:T(8,128)(2,1)S(1)} %get-tuple-element.72), channel_id=1, source_target_pairs={{0,26},{1,27},{2,24},{3,25},{4,30},{5,31},{6,28},{7,29},{8,18},{9,... | collective-permute-start | bytes 393224 | tf_op jit(solution)/shard_map/ppermute | solution.py:419
  46.0 8.3 %collective-permute-start.34 = (bf16[2,128,256]{2,1,0:T(8,128)(2,1)S(1)}, bf16[2,128,256]{2,1,0:T(8,128)(2,1)S(1)}, u32[]{:S(2)}, u32[]{:S(2)}) collective-permute-start(bf16[2,128,256]{2,1,0:T(8,128)(2,1)S(1)} %get-tuple-element.73), channel_id=1, source_target_pairs={{0,27},{1,26},{2,25},{3,24},{4,31},{5,30},{6,29},{7,28},{8,19},{9,... | collective-permute-start | bytes 393224 | tf_op jit(solution)/shard_map/ppermute | solution.py:419
  47.0 11.0 %collective-permute-start.22 = (bf16[2,128,256]{2,1,0:T(8,128)(2,1)S(1)}, bf16[2,128,256]{2,1,0:T(8,128)(2,1)S(1)}, u32[]{:S(2)}, u32[]{:S(2)}) collective-permute-start(bf16[2,128,256]{2,1,0:T(8,128)(2,1)S(1)} %get-tuple-element.43.rest_0_), channel_id=1, source_target_pairs={{0,9},{1,8},{2,11},{3,10},{4,13},{5,12},{6,15},{7,14},{8,1},{9,0},... | collective-permute-start | bytes 393224 | tf_op jit(solution)/shard_map/ppermute | solution.py:419
  48.9 12.0 %collective-permute-start.23 = (bf16[2,128,256]{2,1,0:T(8,128)(2,1)S(1)}, bf16[2,128,256]{2,1,0:T(8,128)(2,1)S(1)}, u32[]{:S(2)}, u32[]{:S(2)}) collective-permute-start(bf16[2,128,256]{2,1,0:T(8,128)(2,1)S(1)} %get-tuple-element.63), channel_id=1, source_target_pairs={{0,15},{1,14},{2,13},{3,12},{4,11},{5,10},{6,9},{7,8},{8,7},{9,6},... | collective-permute-start | bytes 393224 | tf_op jit(solution)/shard_map/ppermute | solution.py:419
  50.2 13.4 %collective-permute-start.24 = (bf16[2,128,256]{2,1,0:T(8,128)(2,1)S(1)}, bf16[2,128,256]{2,1,0:T(8,128)(2,1)S(1)}, u32[]{:S(2)}, u32[]{:S(2)}) collective-permute-start(bf16[2,128,256]{2,1,0:T(8,128)(2,1)S(1)} %get-tuple-element.64), channel_id=1, source_target_pairs={{0,10},{1,11},{2,8},{3,9},{4,14},{5,15},{6,12},{7,13},{8,2},{9,3},... | collective-permute-start | bytes 393224 | tf_op jit(solution)/shard_map/ppermute | solution.py:419
  52.9 13.6 %collective-permute-start.25 = (bf16[2,128,256]{2,1,0:T(8,128)(2,1)S(1)}, bf16[2,128,256]{2,1,0:T(8,128)(2,1)S(1)}, u32[]{:S(2)}, u32[]{:S(2)}) collective-permute-start(bf16[2,128,256]{2,1,0:T(8,128)(2,1)S(1)} %get-tuple-element.65), channel_id=1, source_target_pairs={{0,20},{1,21},{2,22},{3,23},{4,16},{5,17},{6,18},{7,19},{8,28},{9,... | collective-permute-start | bytes 393224 | tf_op jit(solution)/shard_map/ppermute | solution.py:419
  54.3 16.6 %collective-permute-start.26 = (bf16[2,128,256]{2,1,0:T(8,128)(2,1)S(1)}, bf16[2,128,256]{2,1,0:T(8,128)(2,1)S(1)}, u32[]{:S(2)}, u32[]{:S(2)}) collective-permute-start(bf16[2,128,256]{2,1,0:T(8,128)(2,1)S(1)} %get-tuple-element.66), channel_id=1, source_target_pairs={{0,11},{1,10},{2,9},{3,8},{4,15},{5,14},{6,13},{7,12},{8,3},{9,2},... | collective-permute-start | bytes 393224 | tf_op jit(solution)/shard_map/ppermute | solution.py:419
  58.0 12.9 %collective-permute-start.27 = (bf16[2,128,256]{2,1,0:T(8,128)(2,1)S(1)}, bf16[2,128,256]{2,1,0:T(8,128)(2,1)S(1)}, u32[]{:S(2)}, u32[]{:S(2)}) collective-permute-start(bf16[2,128,256]{2,1,0:T(8,128)(2,1)S(1)} %get-tuple-element.67), channel_id=1, source_target_pairs={{0,16},{1,17},{2,18},{3,19},{4,20},{5,21},{6,22},{7,23},{8,24},{9,... | collective-permute-start | bytes 393224 | tf_op jit(solution)/shard_map/ppermute | solution.py:419
  60.9 10.4 %collective-permute-start.28 = (bf16[2,128,256]{2,1,0:T(8,128)(2,1)S(1)}, bf16[2,128,256]{2,1,0:T(8,128)(2,1)S(1)}, u32[]{:S(2)}, u32[]{:S(2)}) collective-permute-start(bf16[2,128,256]{2,1,0:T(8,128)(2,1)S(1)} %get-tuple-element.68), channel_id=1, source_target_pairs={{0,17},{1,16},{2,19},{3,18},{4,21},{5,20},{6,23},{7,22},{8,25},{9,... | collective-permute-start | bytes 393224 | tf_op jit(solution)/shard_map/ppermute | solution.py:419
  63.6 9.5 %collective-permute-start.29 = (bf16[2,128,256]{2,1,0:T(8,128)(2,1)S(1)}, bf16[2,128,256]{2,1,0:T(8,128)(2,1)S(1)}, u32[]{:S(2)}, u32[]{:S(2)}) collective-permute-start(bf16[2,128,256]{2,1,0:T(8,128)(2,1)S(1)} %get-tuple-element.69), channel_id=1, source_target_pairs={{0,18},{1,19},{2,16},{3,17},{4,22},{5,23},{6,20},{7,21},{8,26},{9,... | collective-permute-start | bytes 393224 | tf_op jit(solution)/shard_map/ppermute | solution.py:419
  66.5 15.6 %collective-permute-start.14 = (bf16[2,128,256]{2,1,0:T(8,128)(2,1)S(1)}, bf16[2,128,256]{2,1,0:T(8,128)(2,1)S(1)}, u32[]{:S(2)}, u32[]{:S(2)}) collective-permute-start(bf16[2,128,256]{2,1,0:T(8,128)(2,1)S(1)} %get-tuple-element.42.rest_0_), channel_id=1, source_target_pairs={{0,1},{1,0},{2,3},{3,2},{4,5},{5,4},{6,7},{7,6},{8,9},{9,8},{10,11... | collective-permute-start | bytes 393224 | tf_op jit(solution)/shard_map/ppermute | solution.py:419
  70.9 6.9 %collective-permute-start.30 = (bf16[2,128,256]{2,1,0:T(8,128)(2,1)S(1)}, bf16[2,128,256]{2,1,0:T(8,128)(2,1)S(1)}, u32[]{:S(2)}, u32[]{:S(2)}) collective-permute-start(bf16[2,128,256]{2,1,0:T(8,128)(2,1)S(1)} %get-tuple-element.70), channel_id=1, source_target_pairs={{0,19},{1,18},{2,17},{3,16},{4,23},{5,22},{6,21},{7,20},{8,27},{9,... | collective-permute-start | bytes 393224 | tf_op jit(solution)/shard_map/ppermute | solution.py:419
  71.0 7.8 %collective-permute-start.31 = (bf16[2,128,256]{2,1,0:T(8,128)(2,1)S(1)}, bf16[2,128,256]{2,1,0:T(8,128)(2,1)S(1)}, u32[]{:S(2)}, u32[]{:S(2)}) collective-permute-start(bf16[2,128,256]{2,1,0:T(8,128)(2,1)S(1)} %get-tuple-element.71), channel_id=1, source_target_pairs={{0,24},{1,25},{2,26},{3,27},{4,28},{5,29},{6,30},{7,31},{8,16},{9,... | collective-permute-start | bytes 393224 | tf_op jit(solution)/shard_map/ppermute | solution.py:419
  71.3 10.9 %collective-permute-start.15 = (bf16[2,128,256]{2,1,0:T(8,128)(2,1)S(1)}, bf16[2,128,256]{2,1,0:T(8,128)(2,1)S(1)}, u32[]{:S(2)}, u32[]{:S(2)}) collective-permute-start(bf16[2,128,256]{2,1,0:T(8,128)(2,1)S(1)} %get-tuple-element.56), channel_id=1, source_target_pairs={{0,7},{1,6},{2,5},{3,4},{4,3},{5,2},{6,1},{7,0},{8,15},{9,14},{10,... | collective-permute-start | bytes 393224 | tf_op jit(solution)/shard_map/ppermute | solution.py:419
  73.1 14.2 %collective-permute-start.16 = (bf16[2,128,256]{2,1,0:T(8,128)(2,1)S(1)}, bf16[2,128,256]{2,1,0:T(8,128)(2,1)S(1)}, u32[]{:S(2)}, u32[]{:S(2)}) collective-permute-start(bf16[2,128,256]{2,1,0:T(8,128)(2,1)S(1)} %get-tuple-element.57), channel_id=1, source_target_pairs={{0,2},{1,3},{2,0},{3,1},{4,6},{5,7},{6,4},{7,5},{8,10},{9,11},{10,... | collective-permute-start | bytes 393224 | tf_op jit(solution)/shard_map/ppermute | solution.py:419
  77.8 10.2 %collective-permute-start.17 = (bf16[2,128,256]{2,1,0:T(8,128)(2,1)S(1)}, bf16[2,128,256]{2,1,0:T(8,128)(2,1)S(1)}, u32[]{:S(2)}, u32[]{:S(2)}) collective-permute-start(bf16[2,128,256]{2,1,0:T(8,128)(2,1)S(1)} %get-tuple-element.58), channel_id=1, source_target_pairs={{0,12},{1,13},{2,14},{3,15},{4,8},{5,9},{6,10},{7,11},{8,4},{9,5},... | collective-permute-start | bytes 393224 | tf_op jit(solution)/shard_map/ppermute | solution.py:419
  78.7 10.5 %collective-permute-start.18 = (bf16[2,128,256]{2,1,0:T(8,128)(2,1)S(1)}, bf16[2,128,256]{2,1,0:T(8,128)(2,1)S(1)}, u32[]{:S(2)}, u32[]{:S(2)}) collective-permute-start(bf16[2,128,256]{2,1,0:T(8,128)(2,1)S(1)} %get-tuple-element.59), channel_id=1, source_target_pairs={{0,3},{1,2},{2,1},{3,0},{4,7},{5,6},{6,5},{7,4},{8,11},{9,10},{10,... | collective-permute-start | bytes 393224 | tf_op jit(solution)/shard_map/ppermute | solution.py:419
  82.2 21.9 %collective-permute-start.19 = (bf16[2,128,256]{2,1,0:T(8,128)(2,1)S(1)}, bf16[2,128,256]{2,1,0:T(8,128)(2,1)S(1)}, u32[]{:S(2)}, u32[]{:S(2)}) collective-permute-start(bf16[2,128,256]{2,1,0:T(8,128)(2,1)S(1)} %get-tuple-element.60), channel_id=1, source_target_pairs={{0,13},{1,12},{2,15},{3,14},{4,9},{5,8},{6,11},{7,10},{8,5},{9,4},... | collective-permute-start | bytes 393224 | tf_op jit(solution)/shard_map/ppermute | solution.py:419
  82.2 23.0 %collective-permute-start.20 = (bf16[2,128,256]{2,1,0:T(8,128)(2,1)S(1)}, bf16[2,128,256]{2,1,0:T(8,128)(2,1)S(1)}, u32[]{:S(2)}, u32[]{:S(2)}) collective-permute-start(bf16[2,128,256]{2,1,0:T(8,128)(2,1)S(1)} %get-tuple-element.61), channel_id=1, source_target_pairs={{0,8},{1,9},{2,10},{3,11},{4,12},{5,13},{6,14},{7,15},{8,0},{9,1},... | collective-permute-start | bytes 393224 | tf_op jit(solution)/shard_map/ppermute | solution.py:419
  87.3 18.1 %collective-permute-start.21 = (bf16[2,128,256]{2,1,0:T(8,128)(2,1)S(1)}, bf16[2,128,256]{2,1,0:T(8,128)(2,1)S(1)}, u32[]{:S(2)}, u32[]{:S(2)}) collective-permute-start(bf16[2,128,256]{2,1,0:T(8,128)(2,1)S(1)} %get-tuple-element.62), channel_id=1, source_target_pairs={{0,14},{1,15},{2,12},{3,13},{4,10},{5,11},{6,8},{7,9},{8,6},{9,7},... | collective-permute-start | bytes 393224 | tf_op jit(solution)/shard_map/ppermute | solution.py:419
  88.0 29.8 %collective-permute-start.11 = (bf16[2,128,256]{2,1,0:T(8,128)(2,1)}, bf16[2,128,256]{2,1,0:T(8,128)(2,1)S(1)}, u32[]{:S(2)}, u32[]{:S(2)}) collective-permute-start(bf16[2,128,256]{2,1,0:T(8,128)(2,1)} %get-tuple-element.41.rest_0_), channel_id=1, source_target_pairs={{0,4},{1,5},{2,6},{3,7},{4,0},{5,1},{6,2},{7,3},{8,12},{9,13},{10,... | collective-permute-start | bytes 393224 | tf_op jit(solution)/shard_map/ppermute | solution.py:419
  89.3 31.4 %collective-permute-start.12 = (bf16[2,128,256]{2,1,0:T(8,128)(2,1)}, bf16[2,128,256]{2,1,0:T(8,128)(2,1)S(1)}, u32[]{:S(2)}, u32[]{:S(2)}) collective-permute-start(bf16[2,128,256]{2,1,0:T(8,128)(2,1)} %get-tuple-element.54), channel_id=1, source_target_pairs={{0,5},{1,4},{2,7},{3,6},{4,1},{5,0},{6,3},{7,2},{8,13},{9,12},{10,... | collective-permute-start | bytes 393224 | tf_op jit(solution)/shard_map/ppermute | solution.py:419
  104.1 18.6 %collective-permute-start.13 = (bf16[2,128,256]{2,1,0:T(8,128)(2,1)}, bf16[2,128,256]{2,1,0:T(8,128)(2,1)}, u32[]{:S(2)}, u32[]{:S(2)}) collective-permute-start(bf16[2,128,256]{2,1,0:T(8,128)(2,1)} %get-tuple-element.55), channel_id=1, source_target_pairs={{0,6},{1,7},{2,4},{3,5},{4,2},{5,3},{6,0},{7,1},{8,14},{9,15},{10,... | collective-permute-start | bytes 393224 | tf_op jit(solution)/shard_map/ppermute | solution.py:419
  105.2 25.7 %collective-permute-start.10 = (bf16[2,128,256]{2,1,0:T(8,128)(2,1)}, bf16[2,128,256]{2,1,0:T(8,128)(2,1)S(1)}, u32[]{:S(2)}, u32[]{:S(2)}) collective-permute-start(bf16[2,128,256]{2,1,0:T(8,128)(2,1)} %smooth.9), channel_id=1, source_target_pairs={{0,31},{1,30},{2,29},{3,28},{4,27},{5,26},{6,25},{7,24},{8,23},{9,... | collective-permute-start | bytes 393224 | tf_op jit(solution)/shard_map/ppermute | solution.py:419
  105.4 33.0 %collective-permute-start.4 = (bf16[2,128,256]{2,1,0:T(8,128)(2,1)}, bf16[2,128,256]{2,1,0:T(8,128)(2,1)S(1)}, u32[]{:S(2)}, u32[]{:S(2)}) collective-permute-start(bf16[2,128,256]{2,1,0:T(8,128)(2,1)} %get-tuple-element.47), channel_id=1, source_target_pairs={{0,21},{1,20},{2,23},{3,22},{4,17},{5,16},{6,19},{7,18},{8,29},{9,... | collective-permute-start | bytes 393224 | tf_op jit(solution)/shard_map/ppermute | solution.py:419
  117.8 39.5 %collective-permute-start.5 = (bf16[2,128,256]{2,1,0:T(8,128)(2,1)}, bf16[2,128,256]{2,1,0:T(8,128)(2,1)S(1)}, u32[]{:S(2)}, u32[]{:S(2)}) collective-permute-start(bf16[2,128,256]{2,1,0:T(8,128)(2,1)} %copy-done.3), channel_id=1, source_target_pairs={{0,22},{1,23},{2,20},{3,21},{4,18},{5,19},{6,16},{7,17},{8,30},{9,... | collective-permute-start | bytes 393224 | tf_op jit(solution)/shard_map/ppermute | solution.py:419
  120.7 36.6 %collective-permute-start.6 = (bf16[2,128,256]{2,1,0:T(8,128)(2,1)}, bf16[2,128,256]{2,1,0:T(8,128)(2,1)S(1)}, u32[]{:S(2)}, u32[]{:S(2)}) collective-permute-start(bf16[2,128,256]{2,1,0:T(8,128)(2,1)} %copy-done.2), channel_id=1, source_target_pairs={{0,23},{1,22},{2,21},{3,20},{4,19},{5,18},{6,17},{7,16},{8,31},{9,... | collective-permute-start | bytes 393224 | tf_op jit(solution)/shard_map/ppermute | solution.py:419
  122.6 34.7 %collective-permute-start.7 = (bf16[2,128,256]{2,1,0:T(8,128)(2,1)}, bf16[2,128,256]{2,1,0:T(8,128)(2,1)S(1)}, u32[]{:S(2)}, u32[]{:S(2)}) collective-permute-start(bf16[2,128,256]{2,1,0:T(8,128)(2,1)} %copy-done.1), channel_id=1, source_target_pairs={{0,28},{1,29},{2,30},{3,31},{4,24},{5,25},{6,26},{7,27},{8,20},{9,... | collective-permute-start | bytes 393224 | tf_op jit(solution)/shard_map/ppermute | solution.py:419
  130.9 26.5 %collective-permute-start.8 = (bf16[2,128,256]{2,1,0:T(8,128)(2,1)}, bf16[2,128,256]{2,1,0:T(8,128)(2,1)S(1)}, u32[]{:S(2)}, u32[]{:S(2)}) collective-permute-start(bf16[2,128,256]{2,1,0:T(8,128)(2,1)} %copy-done), channel_id=1, source_target_pairs={{0,29},{1,28},{2,31},{3,30},{4,25},{5,24},{6,27},{7,26},{8,21},{9,... | collective-permute-start | bytes 393224 | tf_op jit(solution)/shard_map/ppermute | solution.py:419
  138.4 18.9 %collective-permute-start.9 = (bf16[2,128,256]{2,1,0:T(8,128)(2,1)S(1)}, bf16[2,128,256]{2,1,0:T(8,128)(2,1)S(1)}, u32[]{:S(2)}, u32[]{:S(2)}) collective-permute-start(bf16[2,128,256]{2,1,0:T(8,128)(2,1)S(1)} %get-tuple-element.52), channel_id=1, source_target_pairs={{0,30},{1,31},{2,28},{3,29},{4,26},{5,27},{6,24},{7,25},{8,22},{9,... | collective-permute-start | bytes 393224 | tf_op jit(solution)/shard_map/ppermute | solution.py:419
